TPU v7x, 32 devices: a whole 2x2x4 slice. The times are simulated.
32 devices in a mesh: row: 4 (over y, core), col: 8 (over z, x).
Axes of the slice: x: 2, y: 2, z: 4, core: 2. Of those that a mesh axis runs over, the one named last changes fastest.
Arguments:
- transition: bfloat16 [6144, 6144], P('row', 'col'), may hold values from 0 to 51.031036, as said below
- tile_pattern: int32 [48, 48], P('row', 'col'), may hold values from 0 to 1, as said below
- kept_tiles: int32 [48, 24], P('row', 'col'), may hold values from 0 to 1, as said below
Outputs:
- next_panel: float32 [6144, 3072], P('row', 'col')
- chaos: float32 [], replicated
Inputs may be any that keep to these rules, and one draw needn't show every extreme that they name: `tile_pattern`: each device's block of 12 x 6 tiles holds at most 36 nonzero tiles, and some block holds exactly 36. Every diagonal tile is nonzero. `kept_tiles`: for panel tile column p, the tile in tile row (p // 3) * 6 + p % 3 is always kept. `transition`: all entries are positive.
All inputs are finite; a program needn't handle non-finite values.
Results may differ from a plain program's by a relative error of at most 0.0003.
Values may be sent and summed in bfloat16 or wider, within the bound.
No kernel may reach another device: no remote copies, remote signals or barrier semaphores. Data moves between devices by JAX's collectives and lax.ppermute only.
A program may use at most 128 MiB of HBM per device.

v0:
```python
import jax
import jax.numpy as jnp
from jax import lax
from jax.sharding import PartitionSpec as P


def expand_tiles(tile_mask, tile_size):
    return jnp.repeat(jnp.repeat(tile_mask, tile_size, axis=0), tile_size, axis=1)


def body(transition, tile_pattern, kept_tiles):
    row_tiles, col_tiles = tile_pattern.shape
    tile_size = transition.shape[0] // row_tiles
    panel_cols = kept_tiles.shape[1]
    width = panel_cols * tile_size
    masked = transition * expand_tiles(tile_pattern, tile_size).astype(jnp.bfloat16)
    own_panel = masked[:, :width]
    column_panel = lax.all_gather(own_panel, "row", axis=0, tiled=True)
    product = jnp.dot(
        lax.all_gather(masked, "col", axis=1, tiled=True),
        column_panel,
        preferred_element_type=jnp.float32,
    )
    pruned = product * expand_tiles(kept_tiles, tile_size).astype(jnp.float32)
    inflated = pruned * pruned
    col_sums, squares = lax.psum(
        (jnp.sum(inflated, axis=0), jnp.sum(inflated * inflated, axis=0)), "row"
    )
    normalized = inflated / col_sums
    spread = squares / (col_sums * col_sums)
    node_count = transition.shape[0] * lax.axis_size("row")
    col_peaks = lax.pmax(jnp.max(inflated, axis=0), "row")
    local_max = jnp.max(col_peaks / col_sums - spread)
    chaos_value = lax.pmax(local_max, "col")
    return (normalized * node_count, chaos_value * node_count)


def solution(mesh):
    placed = (P("row", "col"), P("row", "col"), P("row", "col"))
    return jax.shard_map(
        body, mesh=mesh, in_specs=placed, out_specs=(P("row", "col"), P()), check_vma=False
    )
```

profile of v0, /device:TPU:0, one launch (start us, length us, event | category | flops | bytes accessed | tf_op | source)
XLA Modules:
  0.0 479.7 jit_solution(16388772449998714295)
XLA Ops:
  7.2 0.0 all-gather.5.cloned.1.call-start
  7.2 0.7 convert_element_type.22
  7.9 0.1 broadcast_bitcast_fusion.1
  8.0 4.3 copy.7
  12.3 1.8 bitcast_multiply_fusion
  14.1 0.0 copy-start
  14.1 1.2 slice.4
  15.3 0.0 copy-start.1
  15.3 0.0 all-gather.5.cloned.1.call-update
  15.3 0.0 all-gather.3.cloned.1.call-start
  15.4 0.6 copy-done
  16.0 0.1 all-gather.3.cloned.1.call-update
  16.1 0.0 copy-done.1
  16.1 0.1 broadcast_bitcast_fusion
  16.2 0.3 broadcast_in_dim.16
  16.5 2.0 copy.8
  18.4 37.2 %all-gather.5.cloned.1.call-done = bf16[6144,384]{0,1:T(8,128)(2,1)} async-done(((bf16[1536,384]{0,1:T(8,128)(2,1)}), bf16[6144,384]{0,1:T(8,128)(2,1)}) %all-gather.5.cloned.1.call-update) | async-done | bytes 4718608 | tf_op jit(solution)/shard_map/all_gather | solution.py:18
  55.6 364.0 %all-gather.3.cloned.1.call-done = bf16[1536,6144]{0,1:T(8,128)(2,1)} async-done(((bf16[1536,768]{0,1:T(8,128)(2,1)}), bf16[1536,6144]{0,1:T(8,128)(2,1)}) %all-gather.3.cloned.1.call-update) | async-done | bytes 18874384 | tf_op jit(solution)/shard_map/all_gather | solution.py:20
  419.6 15.6 %fusion.1 = (f32[384]{0:T(512)S(1)}, f32[384]{0:T(512)S(1)}, f32[384]{0:T(512)S(1)}, f32[1536,384]{1,0:T(8,128)S(1)}) fusion(f32[1536,384]{1,0:T(8,128)} %copy.8, bf16[1536,6144]{0,1:T(8,128)(2,1)} %all-gather.3.cloned.1.call-done, bf16[6144,384]{0,1:T(8,128)(2,1)} %all-gather.5.cloned.1.call-done), kind=kOutput, calls=%fused_computation.10 | convolution fusion | flops 7251294720 | bytes 28316160 | tf_op jit(solution)/shard_map/dot_general | solution.py:19
  435.2 6.4 %pmax.14 = f32[384]{0:T(512)S(1)} all-reduce(f32[384]{0:T(512)S(1)} %get-tuple-element.2), channel_id=1, replica_groups=mesh['row'=4,'col'=8] {'row'}, use_global_device_ids=true, to_apply=%region_3.0 | all-reduce | flops 384 | bytes 3072 | tf_op jit(solution)/shard_map/pmax | solution.py:32
  441.6 5.8 %all-reduce = (f32[384]{0:T(512)S(1)}, f32[384]{0:T(512)S(1)}) all-reduce(f32[384]{0:T(512)S(1)} %get-tuple-element.4, f32[384]{0:T(512)S(1)} %get-tuple-element.3), channel_id=1, replica_groups=mesh['row'=4,'col'=8] {'row'}, use_global_device_ids=true, to_apply=%region_1.0 | all-reduce | flops 768 | bytes 6144 | tf_op jit(solution)/shard_map/psum | solution.py:26
  447.5 0.6 subtract_reduce_fusion
  448.1 21.4 %pmax.15 = f32[]{:T(128)} all-reduce(f32[]{:T(128)} %subtract_reduce_fusion), channel_id=1, replica_groups=mesh['row'=4,'col'=8] {'col'}, use_global_device_ids=true, to_apply=%region_7.0 | all-reduce | flops 1 | bytes 8 | tf_op jit(solution)/shard_map/pmax | solution.py:34
  469.5 1.6 divide_multiply_fusion
  (3 shorter events, 0.0 us)
Async XLA Ops:
  7.2 48.5 %all-gather.5.cloned.1.call-start = ((), (), s32[]{:S(2)}) async-start(), calls=%async_computation.1 | async-start | bytes 5898240 | tf_op jit(solution)/shard_map/all_gather | solution.py:18
  14.1 1.9 copy-start
  15.3 0.8 copy-start.1
  15.3 404.3 %all-gather.3.cloned.1.call-start = ((), (), s32[]{:S(2)}) async-start(), calls=%async_computation | async-start | bytes 21233664 | tf_op jit(solution)/shard_map/all_gather | solution.py:20
Sparse Core Ops, SparseCore 0:
  15.5 40.1 all-gather.4
  57.2 362.3 all-gather.2
where the time goes:
time: 480 us
  waiting for transfers between devices  401 us (84%)
  blocking collectives  33.6 us (7%)
  between operations  15.9 us (3%)
  matrix products  15.6 us (3%)
  local copies, waits for them, and re-layouts  8.45 us (2%)
    all_gather x1, waiting for transfers between devices, body(): lax.all_gather(masked, 'col', axis=1, tiled=True)  364 us
    all_gather x1, waiting for transfers between devices, body(): column_panel = lax.all_gather(own_panel, 'row', axis=0, tiled=True)  37.2 us
    pmax x1, blocking collectives, body(): chaos_value = lax.pmax(local_max, 'col')  21.4 us
    dot_general x1, matrix products, body(): jnp.dot(lax.all_gather(masked, 'col', axis=1, tiled=True), column_panel,...  15.6 us
  transfers between devices with their start and end apart: 2, of which 2 were waited for; matrix products, arithmetic and copies ran while one was open for 0% of the time, Pallas kernels for 0%

commit v1 on v0

v1 whole, which is shorter than its diff:
```python
import numpy as np
import jax
import jax.numpy as jnp
from jax import lax
from jax.experimental import pallas as pl
from jax.experimental.pallas import tpu as pltpu
from jax.sharding import PartitionSpec as P


NOTE = 16


def split_axis(size):
    minor = 1
    while minor * minor * 4 <= size:
        minor *= 2
    return size // minor, minor


def pack_tiles(transition, tile_pattern, width):
    rows, cols = transition.shape
    row_tiles, col_tiles = tile_pattern.shape
    t = rows // row_tiles
    half = row_tiles * col_tiles // 4
    half_rows = half * t + NOTE

    def kernel(pat_ref, x_ref, out_ref, panel_ref):
        n = jnp.int32(0)
        lane = lax.broadcasted_iota(jnp.int32, (NOTE, t), 1)
        note = jnp.zeros((NOTE, t), jnp.float32)
        for i in range(row_tiles):
            for k in range(col_tiles):
                on = pat_ref[i, k] > 0
                at = pl.multiple_of(n * t + jnp.where(n >= half, NOTE, 0), NOTE)

                @pl.when(on & (n < 2 * half))
                def _(i=i, k=k, at=at):
                    out_ref[pl.ds(at, t), :] = x_ref[i * t:(i + 1) * t, k * t:(k + 1) * t]

                if (k + 1) * t <= width:
                    tile = x_ref[i * t:(i + 1) * t, k * t:(k + 1) * t]
                    panel_ref[i * t:(i + 1) * t, k * t:(k + 1) * t] = jnp.where(on, tile, jnp.zeros_like(tile))
                note = jnp.where(lane == i * col_tiles + k, on.astype(jnp.float32), note)
                n = n + on.astype(jnp.int32)
        for h in range(2):
            out_ref[h * half_rows + half * t:(h + 1) * half_rows, :] = note.astype(out_ref.dtype)

    return pl.pallas_call(
        kernel,
        out_shape=(
            jax.ShapeDtypeStruct((2 * half_rows, t), transition.dtype),
            jax.ShapeDtypeStruct((rows, width), transition.dtype),
        ),
        in_specs=[pl.BlockSpec(memory_space=pltpu.SMEM), pl.BlockSpec(memory_space=pltpu.VMEM)],
        out_specs=(pl.BlockSpec(memory_space=pltpu.VMEM), pl.BlockSpec(memory_space=pltpu.VMEM)),
        cost_estimate=pl.CostEstimate(flops=0, bytes_accessed=2 * rows * cols * 2, transcendentals=0),
        name="pack",
    )(tile_pattern, transition)


def expand(blocks, meta, first, panels, acc, kept, row_tiles, chunk):
    nb = len(blocks)
    _, slab, width = panels.shape
    t = blocks[0][0].shape[1]
    col_tiles = slab // t
    half = row_tiles * col_tiles // 4
    half_rows = half * t + NOTE
    has_acc = acc is not None
    arrays, notes, where = [], [], []
    for block in blocks:
        where.append(len(arrays))
        arrays += block
        notes.append(block[0][half * t:half * t + 8].astype(jnp.int32))
    n_pre = 2 + nb

    def kernel(*refs):
        meta_ref, kept_ref = refs[:2]
        pat_refs = refs[2:n_pre]
        pos = n_pre
        buf_refs = refs[pos:pos + len(arrays)]
        pos += len(arrays)
        panel_refs = refs[pos:pos + nb]
        pos += nb
        acc_ref = refs[pos] if has_acc else None
        pos += has_acc
        out_ref = refs[pos]
        pos += 1
        if kept is not None:
            stat_ref = refs[pos]
            pos += 1
        strip_ref, count_ref = refs[pos], refs[pos + 1]
        g = pl.program_id(0)

        @pl.when(g == 0)
        def _():
            for b in range(nb):
                count_ref[b] = 0

        out_ref[...] = acc_ref[...] if has_acc else jnp.zeros_like(out_ref)
        for b in range(nb):
            @pl.when(meta_ref[first + b, 0] > 0)
            def _(b=b):
                n = count_ref[b]
                for i in range(chunk):
                    for k in range(col_tiles):
                        on = pat_refs[b][0, (g * chunk + i) * col_tiles + k] > 0
                        slot = jnp.minimum(n, 2 * half - 1)
                        if len(blocks[b]) == 1:
                            at = pl.multiple_of(slot * t + jnp.where(slot >= half, NOTE, 0), NOTE)
                            tile = buf_refs[where[b]][pl.ds(at, t), :]
                        else:
                            at = pl.multiple_of(jnp.where(slot >= half, slot - half, slot) * t, NOTE)
                            tile = jnp.where(
                                slot >= half, buf_refs[where[b] + 1][pl.ds(at, t), :], buf_refs[where[b]][pl.ds(at, t), :])
                        strip_ref[i * t:(i + 1) * t, k * t:(k + 1) * t] = jnp.where(on, tile, jnp.zeros_like(tile))
                        n = n + on.astype(jnp.int32)
                count_ref[b] = n
                out_ref[...] += jnp.dot(strip_ref[...], panel_refs[b][...], preferred_element_type=jnp.float32)

        if kept is not None:
            sums, squares, peaks = [], [], []
            for j in range(width // t):
                total = jnp.zeros((8, t), jnp.float32)
                square = jnp.zeros((8, t), jnp.float32)
                peak = jnp.zeros((8, t), jnp.float32)
                for i in range(chunk):
                    keep = kept_ref[g * chunk + i, j].astype(jnp.float32)
                    pruned = out_ref[i * t:(i + 1) * t, j * t:(j + 1) * t] * keep
                    inflated = pruned * pruned
                    out_ref[i * t:(i + 1) * t, j * t:(j + 1) * t] = inflated
                    grouped = inflated.reshape(t // 8, 8, t)
                    total += jnp.sum(grouped, axis=0)
                    square += jnp.sum(grouped * grouped, axis=0)
                    peak = jnp.maximum(peak, jnp.max(grouped, axis=0))
                sums.append(total)
                squares.append(square)
                peaks.append(peak)
            total = jnp.sum(jnp.concatenate(sums, axis=1), axis=0, keepdims=True)
            square = jnp.sum(jnp.concatenate(squares, axis=1), axis=0, keepdims=True)
            peak = jnp.max(jnp.concatenate(peaks, axis=1), axis=0, keepdims=True)

            @pl.when(g == 0)
            def _():
                stat_ref[0:1, :] = total
                stat_ref[1:2, :] = square
                stat_ref[2:3, :] = peak

            @pl.when(g > 0)
            def _():
                stat_ref[0:1, :] += total
                stat_ref[1:2, :] += square
                stat_ref[2:3, :] = jnp.maximum(stat_ref[2:3, :], peak)

    acc_spec = pl.BlockSpec((chunk * t, width), lambda g, *p: (g, 0))
    in_specs = [pl.BlockSpec(a.shape, lambda g, *p: (0, 0)) for a in arrays]
    in_specs += [
        pl.BlockSpec((pl.Squeezed(), slab, width), lambda g, m, *p, b=b: (m[first + b, 1], 0, 0)) for b in range(nb)
    ]
    out_shape = [jax.ShapeDtypeStruct((row_tiles * t, width), jnp.float32)]
    out_specs = [acc_spec]
    args = [*arrays, *[panels] * nb]
    if has_acc:
        in_specs.append(acc_spec)
        args.append(acc)
    if kept is not None:
        out_shape.append(jax.ShapeDtypeStruct((8, width), jnp.float32))
        out_specs.append(pl.BlockSpec((8, width), lambda g, *p: (0, 0)))
    out = pl.pallas_call(
        kernel,
        out_shape=out_shape,
        grid_spec=pltpu.PrefetchScalarGridSpec(
            num_scalar_prefetch=n_pre,
            grid=(row_tiles // chunk,),
            in_specs=in_specs,
            out_specs=out_specs,
            scratch_shapes=[pltpu.VMEM((chunk * t, slab), jnp.bfloat16), pltpu.SMEM((nb,), jnp.int32)],
        ),
        input_output_aliases={n_pre + len(arrays) + nb: 0} if has_acc else {},
        cost_estimate=pl.CostEstimate(
            flops=2 * nb * row_tiles * t * slab * width,
            bytes_accessed=nb * (2 * half_rows * t + slab * width) * 2 + 2 * row_tiles * t * width * 4,
            transcendentals=0,
        ),
        name="expand",
    )(meta, kept if kept is not None else meta, *notes, *args)
    return out if kept is not None else out[0]


def gather_general(packed, major, minor):
    def line(a, step, direction):
        pairs = []
        for i in range(major):
            have = i if direction > 0 else major - 1 - i
            if 0 <= i + direction < major and have >= step - 1:
                pairs += [(i * minor + j, (i + direction) * minor + j) for j in range(minor)]
        return lax.ppermute(a, "col", pairs)

    def turn(a, shift, at):
        return lax.ppermute(a, "col", [(i * minor + j, i * minor + (j + shift) % minor) for i in at for j in range(minor)])

    here = list(range(major))
    waves = [[([packed], here, 0)] + [([turn(packed, s, here)], here, s) for s in range(1, minor)]]
    up = down = packed
    for step in range(1, major):
        up, down = line(up, step, 1), line(down, step, -1)
        below = [i - step if i >= step else -1 for i in here]
        above = [i + step if i + step < major else -1 for i in here]
        waves.append([([up], below, 0), ([down], above, 0)])
        waves.append([
            ([turn(a, s, [i for i in here if at[i] >= 0])], at, s) for a, at in ((up, below), (down, above)) for s in range(1, minor)
        ])
    return waves


def gather_4x2(packed):
    rows = packed.shape[0] // 2

    def z(a, pairs):
        return lax.ppermute(a, "col", [(i * 2 + j, k * 2 + j) for i, k in pairs for j in range(2)])

    def x(a, at):
        return lax.ppermute(a, "col", [(i * 2 + j, i * 2 + 1 - j) for i in at for j in range(2)])

    d1 = z(packed, [(1, 0), (2, 1), (3, 2)])
    u1 = z(packed, [(0, 1), (1, 2), (2, 3)])
    x0 = x(packed, range(4))
    d2 = z(d1, [(1, 0), (2, 1)])
    u2 = z(u1, [(1, 2), (2, 3)])
    xd1 = x(d1, (0, 1))
    xu1 = x(u1, (2, 3))
    e = z(x0, [(0, 1), (3, 2)])
    d3 = z(d2, [(1, 0)])
    u3 = z(u2, [(2, 3)])
    xd2a = x(d2[:rows], (0, 1))
    xu2a = x(u2[:rows], (2, 3))
    xd2b = x(d2[rows:], (0, 1))
    xu2b = x(u2[rows:], (2, 3))
    fd = z(xd2a, [(1, 0)])
    fu = z(xu2a, [(2, 3)])
    xd3b = x(d3[rows:], (0,))
    xu3b = x(u3[rows:], (3,))
    return [
        [([packed], [0, 1, 2, 3], 0), ([x0], [0, 1, 2, 3], 1)],
        [([d1], [1, 2, 3, -1], 0), ([u1], [-1, 0, 1, 2], 0)],
        [([d2], [2, 3, -1, -1], 0), ([u2], [-1, -1, 0, 1], 0)],
        [([xd1], [1, 2, -1, -1], 1), ([xu1], [-1, -1, 1, 2], 1), ([e], [-1, 0, 3, -1], 1)],
        [
            ([d3], [3, -1, -1, -1], 0), ([u3], [-1, -1, -1, 0], 0),
            ([xd2a, xd2b], [2, 3, -1, -1], 1), ([xu2a, xu2b], [-1, -1, 0, 1], 1),
        ],
        [([fd, xd3b], [3, -1, -1, -1], 1), ([fu, xu3b], [-1, -1, -1, 0], 1)],
    ]


def body(transition, tile_pattern, kept_tiles):
    row_tiles, col_tiles = tile_pattern.shape
    t = transition.shape[0] // row_tiles
    width = kept_tiles.shape[1] * t
    n_row, n_col = lax.axis_size("row"), lax.axis_size("col")
    major, minor = split_axis(n_col)
    n_y = n_row // 2
    ratio = row_tiles // col_tiles
    r, c = lax.axis_index("row"), lax.axis_index("col")

    packed, panel = pack_tiles(transition, tile_pattern, width)
    waves = gather_4x2(packed) if (major, minor) == (4, 2) else gather_general(packed, major, minor)

    pieces = []
    for s in range(n_y):
        there = panel if s == 0 else lax.ppermute(
            panel, "row", [(i * 2 + k, (i + s) % n_y * 2 + k) for i in range(n_y) for k in range(2)])
        pieces += [there, lax.ppermute(there, "row", [(i, i ^ 1) for i in range(n_row)])]
    panels = jnp.concatenate(pieces, axis=0).reshape(n_row * ratio, col_tiles * t, width)

    flat = [entry for wave in waves for entry in wave]
    source = jnp.asarray(np.array([at for _, at, _ in flat], np.int32).T)[c // minor]
    col = jnp.maximum(source, 0) * minor + (c % minor - jnp.asarray(np.array([s for _, _, s in flat], np.int32))) % minor
    owner = col // ratio
    place = ((r // 2 - owner // 2) % n_y * 2 + (r + owner) % 2) * ratio + col % ratio
    meta = jnp.stack([(source >= 0).astype(jnp.int32), place], axis=1).astype(jnp.int32)

    acc, first = None, 0
    for w, wave in enumerate(waves):
        last = w == len(waves) - 1
        acc = expand([a for a, _, _ in wave], meta, first, panels, acc, kept_tiles if last else None, row_tiles, 4)
        first += len(wave)
    inflated, stats = acc

    col_sums, squares = lax.psum((stats[0], stats[1]), "row")
    col_peaks = lax.pmax(stats[2], "row")
    normalized = inflated / col_sums
    spread = squares / (col_sums * col_sums)
    node_count = transition.shape[0] * n_row
    local_max = jnp.max(col_peaks / col_sums - spread)
    chaos_value = lax.pmax(local_max, "col")
    return normalized * node_count, chaos_value * node_count


def solution(mesh):
    placed = (P("row", "col"), P("row", "col"), P("row", "col"))
    return jax.shard_map(body, mesh=mesh, in_specs=placed, out_specs=(P("row", "col"), P()), check_vma=False)
```

time: 480 us -> 191 us (0.40)
  waiting for transfers between devices: 401 us -> 29.5 us
  Pallas kernels: 0 us -> 50 us
  starting transfers between devices: 0.08 us -> 39.2 us
  other arithmetic: 4.71 us -> 24.2 us
  matrix products: 15.6 us -> 0 us
  between operations: 15.9 us -> 2.62 us
    all_gather x2 -> x0, waiting for transfers between devices: 401 us -> none  [the longest x1 364 us: body(): lax.all_gather(masked, 'col', axis=1, tiled=True)]
    pallas_call x0 -> x7, Pallas kernels: none -> 50 us  [the longest x6 46 us: expand(): pl.pallas_call(kernel, out_shape=out_shape, grid_spec=pltpu.PrefetchScala...]
    ppermute x0 -> x21, starting transfers between devices: none -> 39.2 us  [the longest x9 18.4 us: z(): lax.ppermute(a, 'col', [(i * 2 + j, k * 2 + j) for i, k in pairs for j in...]
    ppermute x0 -> x21, waiting for transfers between devices: none -> 29.5 us  [the longest x1 18.7 us: body(): lax.ppermute(panel, 'row', [(i * 2 + k, (i + s) % n_y * 2 + k) for i in r...]
    dot_general x1 -> x0, matrix products: 15.6 us -> none  [body(): jnp.dot(lax.all_gather(masked, 'col', axis=1, tiled=True), column_panel,...]
    convert_element_type x2 -> x16, other arithmetic: 0.69 us -> 15.4 us  [the longest x15 15.4 us: expand(): notes.append(block[0][half * t:half * t + 8].astype(jnp.int32))]
    slice x1 -> x5, local copies, waits for them, and re-layouts: 1.19 us -> 6.29 us  [the longest x1 1.96 us: gather_4x2(): xu3b = x(u3[rows:], (3,))]
    concatenate x0 -> x1, other arithmetic: none -> 4.87 us  [body(): jnp.concatenate(pieces, axis=0).reshape(n_row * ratio, col_tiles * t, width)]
  transfers between devices with their start and end apart: 2 -> 21, of which waited for: 2 -> 4; matrix products, arithmetic and copies ran while one was open for 0% -> 14% of each run, Pallas kernels for 0% -> 20%
where the time goes in v1:
time: 191 us; the launch traced here: 189 us
  Pallas kernels  50 us (26%)
  starting transfers between devices  39.2 us (21%)
  blocking collectives  33.1 us (17%)
  waiting for transfers between devices  29.5 us (15%)
  other arithmetic  24.2 us (13%)
  local copies, waits for them, and re-layouts  10.8 us (6%)
  between operations  2.62 us (1%)
    pallas_call x6, Pallas kernels, expand(): pl.pallas_call(kernel, out_shape=out_shape, grid_spec=pltpu.PrefetchScala...  46 us
    pmax x1, blocking collectives, body(): chaos_value = lax.pmax(local_max, 'col')  20.9 us
    ppermute x1, waiting for transfers between devices, body(): lax.ppermute(panel, 'row', [(i * 2 + k, (i + s) % n_y * 2 + k) for i in r...  18.7 us
    ppermute x9, starting transfers between devices, z(): lax.ppermute(a, 'col', [(i * 2 + j, k * 2 + j) for i, k in pairs for j in...  18.4 us
    ppermute x9, starting transfers between devices, x(): lax.ppermute(a, 'col', [(i * 2 + j, i * 2 + 1 - j) for i in at for j in r...  17.8 us
    convert_element_type x15, other arithmetic, expand(): notes.append(block[0][half * t:half * t + 8].astype(jnp.int32))  15.4 us
    ppermute x9, waiting for transfers between devices, z(): lax.ppermute(a, 'col', [(i * 2 + j, k * 2 + j) for i, k in pairs for j in...  10.8 us
    psum x1, blocking collectives, body(): col_sums, squares = lax.psum((stats[0], stats[1]), 'row')  6.61 us
  transfers between devices with their start and end apart: 21, of which 4 were waited for; matrix products, arithmetic and copies ran while one was open for 14% of the time, Pallas kernels for 20%

profile of v1, /device:TPU:0, one launch (start us, length us, event | category | flops | bytes accessed | tf_op | source)
XLA Modules:
  0.0 189.4 jit_solution(927258098270792064)
XLA Ops:
  0.6 1.4 copy.16.pat_ref
  2.0 3.9 %pack.1 = (bf16[4640,128]{1,0:T(8,128)(2,1)}, bf16[1536,384]{1,0:T(8,128)(2,1)}) custom-call(s32[12,6]{1,0:T(8,128)} %copy.16.pat_ref, bf16[1536,768]{1,0:T(8,128)(2,1)} %x_ref.1), custom_call_target="tpu_custom_call" | custom-call | bytes 4718592 | tf_op jit(solution)/shard_map/pack/pallas_call | solution.py:48
  5.9 3.0 %collective-permute-start.13 = (bf16[1536,384]{1,0:T(8,128)(2,1)}, bf16[1536,384]{1,0:T(8,128)(2,1)S(1)}, u32[]{:S(2)}, u32[]{:S(2)}) collective-permute-start(bf16[1536,384]{1,0:T(8,128)(2,1)} %get-tuple-element.7), channel_id=1, source_target_pairs={{0,16},{8,24},{16,0},{24,8},{1,17},{9,25},{17,1},{25,9},{2,18},{10... | collective-permute-start | bytes 3538952 | tf_op jit(solution)/shard_map/ppermute | solution.py:270
  8.9 4.5 %collective-permute-start.4 = (bf16[4640,128]{1,0:T(8,128)(2,1)}, bf16[4640,128]{1,0:T(8,128)(2,1)}, u32[]{:S(2)}, u32[]{:S(2)}) collective-permute-start(bf16[4640,128]{1,0:T(8,128)(2,1)} %get-tuple-element.6.refs_4_), channel_id=1, source_target_pairs={{0,2},{1,3},{2,4},{3,5},{4,6},{5,7},{8,10},{9,11},{10,12},{11,13},... | collective-permute-start | bytes 3563528 | tf_op jit(solution)/shard_map/ppermute | solution.py:219
  13.5 1.3 collective-permute-start
  14.8 1.6 collective-permute-start.19
  16.4 18.7 %collective-permute-done.13 = bf16[1536,384]{1,0:T(8,128)(2,1)S(1)} collective-permute-done((bf16[1536,384]{1,0:T(8,128)(2,1)}, bf16[1536,384]{1,0:T(8,128)(2,1)S(1)}, u32[]{:S(2)}, u32[]{:S(2)}) %collective-permute-start.13) | collective-permute-done | bytes 1179680 | tf_op jit(solution)/shard_map/ppermute | solution.py:270
  36.5 1.2 slice_convert_fusion.14.refs_2_
  38.6 4.4 %collective-permute-done.refs_4_ = bf16[4640,128]{1,0:T(8,128)(2,1)} collective-permute-done((bf16[4640,128]{1,0:T(8,128)(2,1)}, bf16[4640,128]{1,0:T(8,128)(2,1)}, u32[]{:S(2)}, u32[]{:S(2)}) %collective-permute-start) | collective-permute-done | bytes 1187872 | tf_op jit(solution)/shard_map/ppermute | solution.py:219
  43.0 1.3 collective-permute-start.1
  44.3 1.2 slice_convert_fusion.1.refs_3_
  45.5 1.3 slice_convert_fusion.2.refs_2_
  46.8 1.7 collective-permute-start.18
  48.5 1.3 slice_convert_fusion.refs_3_
  49.8 3.3 %collective-permute-start.17 = (bf16[4640,128]{1,0:T(8,128)(2,1)}, bf16[4640,128]{1,0:T(8,128)(2,1)}, u32[]{:S(2)}, u32[]{:S(2)}) collective-permute-start(bf16[4640,128]{1,0:T(8,128)(2,1)} %collective-permute-done.refs_4_), channel_id=1, source_target_pairs={{0,1},{1,0},{2,3},{3,2},{8,9},{9,8},{10,11},{11,10},{16,17},{17,16... | collective-permute-start | bytes 3563528 | tf_op jit(solution)/shard_map/ppermute | solution.py:222
  53.2 5.6 %collective-permute-start.20 = (bf16[4640,128]{1,0:T(8,128)(2,1)}, bf16[4640,128]{1,0:T(8,128)(2,1)}, u32[]{:S(2)}, u32[]{:S(2)}) collective-permute-start(bf16[4640,128]{1,0:T(8,128)(2,1)} %collective-permute-done.19.refs_5_), channel_id=1, source_target_pairs={{0,2},{1,3},{6,4},{7,5},{8,10},{9,11},{14,12},{15,13},{16,18},{17,... | collective-permute-start | bytes 3563528 | tf_op jit(solution)/shard_map/ppermute | solution.py:219
  58.7 4.9 %pad_maximum_fusion = bf16[6144,384]{1,0:T(8,128)(2,1)} fusion(bf16[1536,384]{1,0:T(8,128)(2,1)} %collective-permute-done.14, bf16[1536,384]{1,0:T(8,128)(2,1)S(1)} %collective-permute-done.13, bf16[1536,384]{1,0:T(8,128)(2,1)} %collective-permute-done.12, bf16[1536,384]{1,0:T(8,128)(2,1)} %get-tuple-element.7), kind=kLoop, calls=%fused_computation | loop fusion | flops 18874368 | bytes 9437184 | tf_op jit(solution)/shard_map/concatenate | solution.py:273
  63.6 7.7 %expand.6.refs_8_ = f32[1536,384]{1,0:T(8,128)} custom-call(s32[15,2]{1,0:T(8,128)} %copy.27.refs_0_.refs_1_, s32[15,2]{1,0:T(8,128)} %copy.27.refs_0_.refs_1_, s32[8,128]{1,0:T(8,128)} %slice_convert_fusion.14.refs_2_, s32[8,128]{1,0:T(8,128)} %slice_convert_fusion.refs_3_, bf16[4640,128]{1,0:T(8,128)(2,1)} %get-tuple-element.6.refs_4_, ...), custom_call_target="tpu_custom_call" | custom-call | flops 1811939328 | bytes 8273920 | tf_op jit(solution)/shard_map/expand/pallas_call | solution.py:168
  71.3 6.9 %expand.7.refs_8_ = f32[1536,384]{1,0:T(8,128)} custom-call(s32[15,2]{1,0:T(8,128)} %copy.27.refs_0_.refs_1_, s32[15,2]{1,0:T(8,128)} %copy.27.refs_0_.refs_1_, s32[8,128]{1,0:T(8,128)} %slice_convert_fusion.2.refs_2_, s32[8,128]{1,0:T(8,128)} %slice_convert_fusion.1.refs_3_, ...), custom_call_target="tpu_custom_call", output_to_operand_aliasing={{}: (8, {})} | custom-call | flops 1811939328 | bytes 8273920 | tf_op jit(solution)/shard_map/expand/pallas_call | solution.py:168
  78.3 1.2 fusion.9
  80.1 1.2 fusion.10
  81.3 2.5 %collective-permute-start.2 = (bf16[2320,128]{1,0:T(8,128)(2,1)}, bf16[2320,128]{1,0:T(8,128)(2,1)}, u32[]{:S(2)}, u32[]{:S(2)}) collective-permute-start(bf16[2320,128]{1,0:T(8,128)(2,1)} %get-tuple-element.18), channel_id=1, source_target_pairs={{0,1},{1,0},{2,3},{3,2},{8,9},{9,8},{10,11},{11,10},{16,17},{17,16... | collective-permute-start | bytes 1781768 | tf_op jit(solution)/shard_map/ppermute | solution.py:222
  85.0 1.7 collective-permute-start.10
  86.7 1.3 slice_convert_fusion.6.refs_3_
  88.0 1.3 collective-permute-start.8
  89.3 1.2 slice_convert_fusion.7.refs_2_
  90.5 3.4 %collective-permute-start.15 = (bf16[2320,128]{1,0:T(8,128)(2,1)}, bf16[2320,128]{1,0:T(8,128)(2,1)}, u32[]{:S(2)}, u32[]{:S(2)}) collective-permute-start(bf16[2320,128]{1,0:T(8,128)(2,1)} %get-tuple-element.17), channel_id=1, source_target_pairs={{0,1},{1,0},{2,3},{3,2},{8,9},{9,8},{10,11},{11,10},{16,17},{17,16... | collective-permute-start | bytes 1781768 | tf_op jit(solution)/shard_map/ppermute | solution.py:222
  93.9 1.3 slice_convert_fusion.5.refs_4_
  95.1 6.9 %expand.8.refs_11_ = f32[1536,384]{1,0:T(8,128)} custom-call(s32[15,2]{1,0:T(8,128)} %copy.27.refs_0_.refs_1_, s32[15,2]{1,0:T(8,128)} %copy.27.refs_0_.refs_1_, s32[8,128]{1,0:T(8,128)} %slice_convert_fusion.4.refs_2_, s32[8,128]{1,0:T(8,128)} %slice_convert_fusion.3.refs_3_, bf16[4640,128]{1,0:T(8,128)(2,1)} %copy-done, ...), custom_call_target="tpu_custom_call", output_to_operand_aliasing={{}: (8, {})} | custom-call | flops 1811939328 | bytes 8273920 | tf_op jit(solution)/shard_map/expand/pallas_call | solution.py:168
  102.1 7.8 %expand.9.refs_16_ = f32[1536,384]{1,0:T(8,128)} custom-call(s32[15,2]{1,0:T(8,128)} %copy.27.refs_0_.refs_1_, s32[15,2]{1,0:T(8,128)} %copy.27.refs_0_.refs_1_, s32[8,128]{1,0:T(8,128)} %slice_convert_fusion.7.refs_2_, s32[8,128]{1,0:T(8,128)} %slice_convert_fusion.6.refs_3_, ...), custom_call_target="tpu_custom_call", output_to_operand_aliasing={{}: (11, {})} | custom-call | flops 2717908992 | bytes 10051584 | tf_op jit(solution)/shard_map/expand/pallas_call | solution.py:168
  109.9 1.5 collective-permute-start.16
  112.7 1.2 slice_convert_fusion.9.refs_4_
  113.9 1.3 collective-permute-start.3
  115.2 2.0 %slice.101 = bf16[2320,128]{1,0:T(8,128)(2,1)} slice(bf16[4640,128]{1,0:T(8,128)(2,1)} %collective-permute-done.10.refs_7_), slice={[2320:4640], [0:128]} | slice | bytes 1187840 | tf_op jit(solution)/shard_map/slice | solution.py:241
  117.8 1.1 slice.100
  119.0 1.2 slice_convert_fusion.10.refs_3_
  120.2 1.2 slice_convert_fusion.11.refs_2_
  121.4 2.5 %collective-permute-start.9 = (bf16[2320,128]{1,0:T(8,128)(2,1)S(1)}, bf16[2320,128]{1,0:T(8,128)(2,1)S(1)}, u32[]{:S(2)}, u32[]{:S(2)}) collective-permute-start(bf16[2320,128]{1,0:T(8,128)(2,1)S(1)} %slice.100), channel_id=1, source_target_pairs={{0,1},{1,0},{8,9},{9,8},{16,17},{17,16},{24,25},{25,24}} | collective-permute-start | bytes 1781768 | tf_op jit(solution)/shard_map/ppermute | solution.py:222
  124.5 6.2 %collective-permute-done.3.refs_4_ = bf16[2320,128]{1,0:T(8,128)(2,1)S(1)} collective-permute-done((bf16[2320,128]{1,0:T(8,128)(2,1)}, bf16[2320,128]{1,0:T(8,128)(2,1)S(1)}, u32[]{:S(2)}, u32[]{:S(2)}) %collective-permute-start.3) | collective-permute-done | bytes 593952 | tf_op jit(solution)/shard_map/ppermute | solution.py:219
  131.4 9.3 %expand.10.refs_10_ = f32[1536,384]{1,0:T(8,128)} custom-call(s32[15,2]{1,0:T(8,128)} %copy.27.refs_0_.refs_1_, s32[15,2]{1,0:T(8,128)} %copy.27.refs_0_.refs_1_, s32[8,128]{1,0:T(8,128)} %slice_convert_fusion.11.refs_2_, s32[8,128]{1,0:T(8,128)} %slice_convert_fusion.10.refs_3_, ...), custom_call_target="tpu_custom_call", output_to_operand_aliasing={{}: (16, {})} | custom-call | flops 3623878656 | bytes 11829248 | tf_op jit(solution)/shard_map/expand/pallas_call | solution.py:168
  140.8 0.8 copy-done.5
  141.6 0.9 copy-done.6
  142.5 7.3 %expand.11 = (f32[1536,384]{1,0:T(8,128)}, f32[8,384]{1,0:T(8,128)}) custom-call(s32[15,2]{1,0:T(8,128)} %copy.27.refs_0_.refs_1_, s32[12,3]{1,0:T(8,128)} %copy.28.refs_1_, s32[8,128]{1,0:T(8,128)} %slice_convert_fusion.13.refs_2_, s32[8,128]{1,0:T(8,128)} %slice_convert_fusion.12.refs_3_, ...), custom_call_target="tpu_custom_call", output_to_operand_aliasing={{0}: (10, {})} | custom-call | flops 1811939328 | bytes 8273920 | tf_op jit(solution)/shard_map/expand/pallas_call | solution.py:168
  149.8 0.8 slice_reduce_fusion.1
  150.6 5.7 %pmax.14 = f32[384]{0:T(512)S(1)} all-reduce(f32[384]{0:T(512)S(1)} %get-tuple-element.10), channel_id=1, replica_groups=mesh['row'=4,'col'=8] {'row'}, use_global_device_ids=true, to_apply=%region_1.2 | all-reduce | flops 384 | bytes 3072 | tf_op jit(solution)/shard_map/pmax | solution.py:290
  156.3 6.6 %all-reduce = (f32[384]{0:T(512)S(1)}, f32[384]{0:T(512)S(1)}) all-reduce(f32[384]{0:T(512)S(1)} %get-tuple-element.12, f32[384]{0:T(512)S(1)} %get-tuple-element.11), channel_id=1, replica_groups=mesh['row'=4,'col'=8] {'row'}, use_global_device_ids=true, to_apply=%region_0.1 | all-reduce | flops 768 | bytes 6144 | tf_op jit(solution)/shard_map/psum | solution.py:289
  163.5 20.9 %pmax.15 = f32[]{:T(128)} all-reduce(f32[]{:T(128)} %subtract_reduce_fusion), channel_id=1, replica_groups=mesh['row'=4,'col'=8] {'col'}, use_global_device_ids=true, to_apply=%region_4.5 | all-reduce | flops 1 | bytes 8 | tf_op jit(solution)/shard_map/pmax | solution.py:295
  184.4 3.2 %divide_multiply_fusion = f32[1536,384]{1,0:T(8,128)} fusion(f32[1536,384]{1,0:T(8,128)} %get-tuple-element.8, f32[384]{0:T(512)S(1)} %get-tuple-element.13), kind=kLoop, calls=%fused_computation.1 | loop fusion | flops 1179648 | bytes 4720128 | tf_op jit(solution)/shard_map/mul | solution.py:296
  (53 shorter events, 8.0 us)
Async XLA Ops:
  2.0 14.4 %copy-start.9 = (s32[4,15]{1,0:T(4,128)S(1)}, s32[4,15]{1,0:T(4,128)}, u32[]{:S(2)}) copy-start(s32[4,15]{1,0:T(4,128)} %constant.92.clone) | copy-start | bytes 724
  2.0 33.1 %copy-start.8 = (s32[15]{0:T(128)S(1)}, s32[15]{0:T(128)}, u32[]{:S(2)}) copy-start(s32[15]{0:T(128)} %constant.96) | copy-start | bytes 184
  2.0 33.8 %copy-start.7 = (s32[12,3]{0,1:T(4,128)S(1)}, s32[12,3]{0,1:T(4,128)}, u32[]{:S(2)}) copy-start(s32[12,3]{0,1:T(4,128)} %param.7) | copy-start | bytes 436
  5.9 29.2 %collective-permute-start.13 = (bf16[1536,384]{1,0:T(8,128)(2,1)}, bf16[1536,384]{1,0:T(8,128)(2,1)S(1)}, u32[]{:S(2)}, u32[]{:S(2)}) collective-permute-start(bf16[1536,384]{1,0:T(8,128)(2,1)} %get-tuple-element.7), channel_id=1, source_target_pairs={{0,16},{8,24},{16,0},{24,8},{1,17},{9,25},{17,1},{25,9},{2,18},{10... | collective-permute-start | bytes 3538952 | tf_op jit(solution)/shard_map/ppermute | solution.py:270
  8.9 28.9 %collective-permute-start.4 = (bf16[4640,128]{1,0:T(8,128)(2,1)}, bf16[4640,128]{1,0:T(8,128)(2,1)}, u32[]{:S(2)}, u32[]{:S(2)}) collective-permute-start(bf16[4640,128]{1,0:T(8,128)(2,1)} %get-tuple-element.6.refs_4_), channel_id=1, source_target_pairs={{0,2},{1,3},{2,4},{3,5},{4,6},{5,7},{8,10},{9,11},{10,12},{11,13},... | collective-permute-start | bytes 3563528 | tf_op jit(solution)/shard_map/ppermute | solution.py:219
  13.5 29.5 %collective-permute-start = (bf16[4640,128]{1,0:T(8,128)(2,1)}, bf16[4640,128]{1,0:T(8,128)(2,1)}, u32[]{:S(2)}, u32[]{:S(2)}) collective-permute-start(bf16[4640,128]{1,0:T(8,128)(2,1)} %get-tuple-element.6.refs_4_), channel_id=1, source_target_pairs={{2,0},{3,1},{4,2},{5,3},{6,4},{7,5},{10,8},{11,9},{12,10},{13,11},... | collective-permute-start | bytes 3563528 | tf_op jit(solution)/shard_map/ppermute | solution.py:219
  14.8 32.0 %collective-permute-start.19 = (bf16[4640,128]{1,0:T(8,128)(2,1)}, bf16[4640,128]{1,0:T(8,128)(2,1)}, u32[]{:S(2)}, u32[]{:S(2)}) collective-permute-start(bf16[4640,128]{1,0:T(8,128)(2,1)} %get-tuple-element.6.refs_4_), channel_id=1, source_target_pairs={{0,1},{1,0},{2,3},{3,2},{4,5},{5,4},{6,7},{7,6},{8,9},{9,8},{10,11... | collective-permute-start | bytes 3563528 | tf_op jit(solution)/shard_map/ppermute | solution.py:222
  16.4 33.4 %collective-permute-start.12 = (bf16[1536,384]{1,0:T(8,128)(2,1)}, bf16[1536,384]{1,0:T(8,128)(2,1)}, u32[]{:S(2)}, u32[]{:S(2)}) collective-permute-start(bf16[1536,384]{1,0:T(8,128)(2,1)} %get-tuple-element.7), channel_id=1, source_target_pairs={{0,8},{8,0},{16,24},{24,16},{1,9},{9,1},{17,25},{25,17},{2,10},{10... | collective-permute-start | bytes 3538952 | tf_op jit(solution)/shard_map/ppermute | solution.py:272
  35.1 18.0 %collective-permute-start.14 = (bf16[1536,384]{1,0:T(8,128)(2,1)S(1)}, bf16[1536,384]{1,0:T(8,128)(2,1)}, u32[]{:S(2)}, u32[]{:S(2)}) collective-permute-start(bf16[1536,384]{1,0:T(8,128)(2,1)S(1)} %collective-permute-done.13), channel_id=1, source_target_pairs={{0,8},{8,0},{16,24},{24,16},{1,9},{9,1},{17,25},{25,17},{2,10},{10... | collective-permute-start | bytes 3538952 | tf_op jit(solution)/shard_map/ppermute | solution.py:272
  37.9 40.4 %collective-permute-start.5 = (bf16[4640,128]{1,0:T(8,128)(2,1)}, bf16[4640,128]{1,0:T(8,128)(2,1)S(1)}, u32[]{:S(2)}, u32[]{:S(2)}) collective-permute-start(bf16[4640,128]{1,0:T(8,128)(2,1)} %collective-permute-done.4.refs_5_), channel_id=1, source_target_pairs={{2,4},{3,5},{4,6},{5,7},{10,12},{11,13},{12,14},{13,15},{18,20},{1... | collective-permute-start | bytes 3563528 | tf_op jit(solution)/shard_map/ppermute | solution.py:219
  43.0 37.1 %collective-permute-start.1 = (bf16[4640,128]{1,0:T(8,128)(2,1)}, bf16[4640,128]{1,0:T(8,128)(2,1)S(1)}, u32[]{:S(2)}, u32[]{:S(2)}) collective-permute-start(bf16[4640,128]{1,0:T(8,128)(2,1)} %collective-permute-done.refs_4_), channel_id=1, source_target_pairs={{2,0},{3,1},{4,2},{5,3},{10,8},{11,9},{12,10},{13,11},{18,16},{19,... | collective-permute-start | bytes 3563528 | tf_op jit(solution)/shard_map/ppermute | solution.py:219
  46.8 38.2 %collective-permute-start.18 = (bf16[4640,128]{1,0:T(8,128)(2,1)}, bf16[4640,128]{1,0:T(8,128)(2,1)}, u32[]{:S(2)}, u32[]{:S(2)}) collective-permute-start(bf16[4640,128]{1,0:T(8,128)(2,1)} %collective-permute-done.4.refs_5_), channel_id=1, source_target_pairs={{4,5},{5,4},{6,7},{7,6},{12,13},{13,12},{14,15},{15,14},{20,21},{2... | collective-permute-start | bytes 3563528 | tf_op jit(solution)/shard_map/ppermute | solution.py:222
  49.8 38.2 %collective-permute-start.17 = (bf16[4640,128]{1,0:T(8,128)(2,1)}, bf16[4640,128]{1,0:T(8,128)(2,1)}, u32[]{:S(2)}, u32[]{:S(2)}) collective-permute-start(bf16[4640,128]{1,0:T(8,128)(2,1)} %collective-permute-done.refs_4_), channel_id=1, source_target_pairs={{0,1},{1,0},{2,3},{3,2},{8,9},{9,8},{10,11},{11,10},{16,17},{17,16... | collective-permute-start | bytes 3563528 | tf_op jit(solution)/shard_map/ppermute | solution.py:222
  53.2 37.3 %collective-permute-start.20 = (bf16[4640,128]{1,0:T(8,128)(2,1)}, bf16[4640,128]{1,0:T(8,128)(2,1)}, u32[]{:S(2)}, u32[]{:S(2)}) collective-permute-start(bf16[4640,128]{1,0:T(8,128)(2,1)} %collective-permute-done.19.refs_5_), channel_id=1, source_target_pairs={{0,2},{1,3},{6,4},{7,5},{8,10},{9,11},{14,12},{15,13},{16,18},{17,... | collective-permute-start | bytes 3563528 | tf_op jit(solution)/shard_map/ppermute | solution.py:219
  78.2 6.7 %copy-start.1 = (bf16[4640,128]{1,0:T(8,128)(2,1)}, bf16[4640,128]{1,0:T(8,128)(2,1)S(1)}, u32[]{:S(2)}) copy-start(bf16[4640,128]{1,0:T(8,128)(2,1)S(1)} %collective-permute-done.5.refs_5_) | copy-start | bytes 3563524
  79.4 30.5 %collective-permute-start.6 = (bf16[2320,128]{1,0:T(8,128)(2,1)}, bf16[2320,128]{1,0:T(8,128)(2,1)S(1)}, u32[]{:S(2)}, u32[]{:S(2)}) collective-permute-start(bf16[2320,128]{1,0:T(8,128)(2,1)} %get-tuple-element.16), channel_id=1, source_target_pairs={{4,5},{5,4},{6,7},{7,6},{12,13},{13,12},{14,15},{15,14},{20,21},{2... | collective-permute-start | bytes 1781768 | tf_op jit(solution)/shard_map/ppermute | solution.py:222
  80.1 7.9 %copy-start = (bf16[4640,128]{1,0:T(8,128)(2,1)}, bf16[4640,128]{1,0:T(8,128)(2,1)S(1)}, u32[]{:S(2)}) copy-start(bf16[4640,128]{1,0:T(8,128)(2,1)S(1)} %collective-permute-done.1.refs_4_) | copy-start | bytes 3563524
  81.3 30.6 %collective-permute-start.2 = (bf16[2320,128]{1,0:T(8,128)(2,1)}, bf16[2320,128]{1,0:T(8,128)(2,1)}, u32[]{:S(2)}, u32[]{:S(2)}) collective-permute-start(bf16[2320,128]{1,0:T(8,128)(2,1)} %get-tuple-element.18), channel_id=1, source_target_pairs={{0,1},{1,0},{2,3},{3,2},{8,9},{9,8},{10,11},{11,10},{16,17},{17,16... | collective-permute-start | bytes 1781768 | tf_op jit(solution)/shard_map/ppermute | solution.py:222
  85.0 28.9 %collective-permute-start.10 = (bf16[4640,128]{1,0:T(8,128)(2,1)S(1)}, bf16[4640,128]{1,0:T(8,128)(2,1)}, u32[]{:S(2)}, u32[]{:S(2)}) collective-permute-start(bf16[4640,128]{1,0:T(8,128)(2,1)S(1)} %collective-permute-done.5.refs_5_), channel_id=1, source_target_pairs={{4,6},{5,7},{12,14},{13,15},{20,22},{21,23},{28,30},{29,31}} | collective-permute-start | bytes 3563528 | tf_op jit(solution)/shard_map/ppermute | solution.py:219
  88.0 29.1 %collective-permute-start.8 = (bf16[4640,128]{1,0:T(8,128)(2,1)S(1)}, bf16[4640,128]{1,0:T(8,128)(2,1)}, u32[]{:S(2)}, u32[]{:S(2)}) collective-permute-start(bf16[4640,128]{1,0:T(8,128)(2,1)S(1)} %collective-permute-done.1.refs_4_), channel_id=1, source_target_pairs={{2,0},{3,1},{10,8},{11,9},{18,16},{19,17},{26,24},{27,25}} | collective-permute-start | bytes 3563528 | tf_op jit(solution)/shard_map/ppermute | solution.py:219
  90.5 40.9 %collective-permute-start.15 = (bf16[2320,128]{1,0:T(8,128)(2,1)}, bf16[2320,128]{1,0:T(8,128)(2,1)}, u32[]{:S(2)}, u32[]{:S(2)}) collective-permute-start(bf16[2320,128]{1,0:T(8,128)(2,1)} %get-tuple-element.17), channel_id=1, source_target_pairs={{0,1},{1,0},{2,3},{3,2},{8,9},{9,8},{10,11},{11,10},{16,17},{17,16... | collective-permute-start | bytes 1781768 | tf_op jit(solution)/shard_map/ppermute | solution.py:222
  109.9 9.1 %copy-start.2 = (bf16[2320,128]{1,0:T(8,128)(2,1)}, bf16[2320,128]{1,0:T(8,128)(2,1)S(1)}, u32[]{:S(2)}) copy-start(bf16[2320,128]{1,0:T(8,128)(2,1)S(1)} %collective-permute-done.6.refs_10_) | copy-start | bytes 1781764
  109.9 21.5 %collective-permute-start.16 = (bf16[2320,128]{1,0:T(8,128)(2,1)}, bf16[2320,128]{1,0:T(8,128)(2,1)}, u32[]{:S(2)}, u32[]{:S(2)}) collective-permute-start(bf16[2320,128]{1,0:T(8,128)(2,1)} %get-tuple-element.15), channel_id=1, source_target_pairs={{4,5},{5,4},{6,7},{7,6},{12,13},{13,12},{14,15},{15,14},{20,21},{2... | collective-permute-start | bytes 1781768 | tf_op jit(solution)/shard_map/ppermute | solution.py:222
  112.0 9.5 %collective-permute-start.7 = (bf16[2320,128]{1,0:T(8,128)(2,1)S(1)}, bf16[2320,128]{1,0:T(8,128)(2,1)S(1)}, u32[]{:S(2)}, u32[]{:S(2)}) collective-permute-start(bf16[2320,128]{1,0:T(8,128)(2,1)S(1)} %collective-permute-done.6.refs_10_), channel_id=1, source_target_pairs={{4,6},{5,7},{12,14},{13,15},{20,22},{21,23},{28,30},{29,31}} | collective-permute-start | bytes 1781768 | tf_op jit(solution)/shard_map/ppermute | solution.py:219
  113.9 16.9 %collective-permute-start.3 = (bf16[2320,128]{1,0:T(8,128)(2,1)}, bf16[2320,128]{1,0:T(8,128)(2,1)S(1)}, u32[]{:S(2)}, u32[]{:S(2)}) collective-permute-start(bf16[2320,128]{1,0:T(8,128)(2,1)} %collective-permute-done.2.refs_8_), channel_id=1, source_target_pairs={{2,0},{3,1},{10,8},{11,9},{18,16},{19,17},{26,24},{27,25}} | collective-permute-start | bytes 1781768 | tf_op jit(solution)/shard_map/ppermute | solution.py:219
  117.1 23.6 %collective-permute-start.11 = (bf16[2320,128]{1,0:T(8,128)(2,1)}, bf16[2320,128]{1,0:T(8,128)(2,1)S(1)}, u32[]{:S(2)}, u32[]{:S(2)}) collective-permute-start(bf16[2320,128]{1,0:T(8,128)(2,1)} %slice.101), channel_id=1, source_target_pairs={{6,7},{7,6},{14,15},{15,14},{22,23},{23,22},{30,31},{31,30}} | collective-permute-start | bytes 1781768 | tf_op jit(solution)/shard_map/ppermute | solution.py:222
  121.4 2.5 %copy-start.3 = (bf16[2320,128]{1,0:T(8,128)(2,1)}, bf16[2320,128]{1,0:T(8,128)(2,1)S(1)}, u32[]{:S(2)}) copy-start(bf16[2320,128]{1,0:T(8,128)(2,1)S(1)} %collective-permute-done.7.refs_6_) | copy-start | bytes 1781764
  121.4 19.3 %collective-permute-start.9 = (bf16[2320,128]{1,0:T(8,128)(2,1)S(1)}, bf16[2320,128]{1,0:T(8,128)(2,1)S(1)}, u32[]{:S(2)}, u32[]{:S(2)}) collective-permute-start(bf16[2320,128]{1,0:T(8,128)(2,1)S(1)} %slice.100), channel_id=1, source_target_pairs={{0,1},{1,0},{8,9},{9,8},{16,17},{17,16},{24,25},{25,24}} | collective-permute-start | bytes 1781768 | tf_op jit(solution)/shard_map/ppermute | solution.py:222
  130.8 10.0 %copy-start.4 = (bf16[2320,128]{1,0:T(8,128)(2,1)}, bf16[2320,128]{1,0:T(8,128)(2,1)S(1)}, u32[]{:S(2)}) copy-start(bf16[2320,128]{1,0:T(8,128)(2,1)S(1)} %collective-permute-done.3.refs_4_) | copy-start | bytes 1781764
  140.7 0.9 copy-start.5
  141.6 0.9 copy-start.6

commit v2 on v0

v2 whole, which is shorter than its diff:
```python
import numpy as np
import jax
import jax.numpy as jnp
from jax import lax
from jax.experimental import pallas as pl
from jax.experimental.pallas import tpu as pltpu
from jax.sharding import PartitionSpec as P


NOTE = 16


def split_axis(size):
    minor = 1
    while minor * minor * 4 <= size:
        minor *= 2
    return size // minor, minor


def pack_tiles(transition, pattern_t, width):
    rows, cols = transition.shape
    col_tiles, row_tiles = pattern_t.shape
    t = rows // row_tiles
    cap = row_tiles * col_tiles // 2

    def kernel(pat_ref, x_ref, out_ref, panel_ref):
        n = jnp.int32(0)
        lane = lax.broadcasted_iota(jnp.int32, (NOTE, t), 1)
        note = jnp.zeros((NOTE, t), jnp.float32)
        for i in range(row_tiles):
            for k in range(col_tiles):
                on = pat_ref[k, i] > 0

                @pl.when(on & (n < cap))
                def _(i=i, k=k, n=n):
                    out_ref[pl.ds(pl.multiple_of(n * t, t), t), :] = x_ref[i * t:(i + 1) * t, k * t:(k + 1) * t]

                if (k + 1) * t <= width:
                    tile = x_ref[i * t:(i + 1) * t, k * t:(k + 1) * t]
                    panel_ref[i * t:(i + 1) * t, k * t:(k + 1) * t] = jnp.where(on, tile, jnp.zeros_like(tile))
                note = jnp.where(lane == i * col_tiles + k, on.astype(jnp.float32), note)
                n = n + on.astype(jnp.int32)
        out_ref[cap * t:cap * t + NOTE, :] = note.astype(out_ref.dtype)

    return pl.pallas_call(
        kernel,
        out_shape=(
            jax.ShapeDtypeStruct((cap * t + NOTE, t), transition.dtype),
            jax.ShapeDtypeStruct((rows, width), transition.dtype),
        ),
        in_specs=[pl.BlockSpec(memory_space=pltpu.SMEM), pl.BlockSpec(memory_space=pltpu.VMEM)],
        out_specs=(pl.BlockSpec(memory_space=pltpu.VMEM), pl.BlockSpec(memory_space=pltpu.VMEM)),
        cost_estimate=pl.CostEstimate(flops=0, bytes_accessed=2 * rows * cols * 2, transcendentals=0),
        name="pack",
    )(pattern_t, transition)


def expand(blocks, meta, first, pieces, acc, kept_t, row_tiles, chunk):
    nb, nq = len(blocks), len(pieces)
    _, slab, width = pieces[0].shape
    t = blocks[0].shape[1]
    col_tiles = slab // t
    cap = row_tiles * col_tiles // 2
    has_acc, last = acc is not None, kept_t is not None

    def kernel(*refs):
        refs = list(refs)
        meta_ref = refs.pop(0)
        kept_ref = refs.pop(0) if last else None
        block_refs, refs = refs[:nb], refs[nb:]
        piece_refs, refs = refs[:nq], refs[nq:]
        acc_ref = refs.pop(0) if has_acc else None
        out_ref = refs.pop(0)
        stat_ref = refs.pop(0) if last else None
        buf_ref, slab_ref, note_ref, pat_ref, strip_ref, buf_sem, slab_sem, pat_sem = refs

        def load(b):
            return pltpu.make_async_copy(block_refs[b], buf_ref.at[b], buf_sem.at[b])

        def load_slab(b, q):
            return pltpu.make_async_copy(piece_refs[q].at[meta_ref[first + b, 2]], slab_ref.at[b], slab_sem.at[b])

        for b in range(nb):
            @pl.when(meta_ref[first + b, 0] > 0)
            def _(b=b):
                load(b).start()
                for q in range(nq):
                    @pl.when(meta_ref[first + b, 1] == q)
                    def _(q=q):
                        load_slab(b, q).start()

        if has_acc:
            out_ref[...] = acc_ref[...]
        else:
            out_ref[...] = jnp.zeros_like(out_ref)

        for b in range(nb):
            @pl.when(meta_ref[first + b, 0] > 0)
            def _(b=b):
                load(b).wait()
                note_ref[...] = buf_ref[b, cap * t:cap * t + 8, :].astype(jnp.float32).astype(jnp.int32)
                to_scalar = pltpu.make_async_copy(note_ref, pat_ref, pat_sem)
                to_scalar.start()
                to_scalar.wait()
                load_slab(b, 0).wait()

                def step(g, n):
                    for i in range(chunk):
                        for k in range(col_tiles):
                            on = pat_ref[0, (g * chunk + i) * col_tiles + k] > 0
                            at = pl.multiple_of(jnp.minimum(n, cap - 1) * t, t)
                            tile = buf_ref[b, pl.ds(at, t), :]
                            strip_ref[i * t:(i + 1) * t, k * t:(k + 1) * t] = jnp.where(on, tile, jnp.zeros_like(tile))
                            n = n + on.astype(jnp.int32)
                    rows = pl.ds(pl.multiple_of(g * chunk * t, t), chunk * t)
                    out_ref[rows, :] += jnp.dot(strip_ref[...], slab_ref[b], preferred_element_type=jnp.float32)
                    return n

                lax.fori_loop(0, row_tiles // chunk, step, jnp.int32(0))

        if last:
            stat_ref[...] = jnp.zeros_like(stat_ref)
            for j in range(width // t):
                cols = slice(j * t, (j + 1) * t)

                def tile_row(i, carry, cols=cols, j=j):
                    total, square, peak = carry
                    rows = pl.ds(pl.multiple_of(i * t, t), t)
                    pruned = out_ref[rows, cols] * kept_ref[j, i].astype(jnp.float32)
                    inflated = pruned * pruned
                    out_ref[rows, cols] = inflated
                    grouped = inflated.reshape(t // 8, 8, t)
                    return (
                        total + jnp.sum(grouped, axis=0),
                        square + jnp.sum(grouped * grouped, axis=0),
                        jnp.maximum(peak, jnp.max(grouped, axis=0)),
                    )

                zero = jnp.zeros((8, t), jnp.float32)
                total, square, peak = lax.fori_loop(0, row_tiles, tile_row, (zero, zero, zero))
                stat_ref[0:1, cols] = jnp.sum(total, axis=0, keepdims=True)
                stat_ref[1:2, cols] = jnp.sum(square, axis=0, keepdims=True)
                stat_ref[2:3, cols] = jnp.max(peak, axis=0, keepdims=True)

    smem, vmem, anywhere = (pl.BlockSpec(memory_space=m) for m in (pltpu.SMEM, pltpu.VMEM, pl.ANY))
    args, in_specs = [meta], [smem]
    if last:
        args.append(kept_t)
        in_specs.append(smem)
    args += [*blocks, *pieces]
    in_specs += [anywhere] * (nb + nq)
    out_shape = [jax.ShapeDtypeStruct((row_tiles * t, width), jnp.float32)]
    if has_acc:
        args.append(acc)
        in_specs.append(vmem)
    if last:
        out_shape.append(jax.ShapeDtypeStruct((8, width), jnp.float32))
    out = pl.pallas_call(
        kernel,
        out_shape=out_shape,
        in_specs=in_specs,
        out_specs=[vmem] * len(out_shape),
        scratch_shapes=[
            pltpu.VMEM((nb, cap * t + NOTE, t), jnp.bfloat16),
            pltpu.VMEM((nb, slab, width), jnp.bfloat16),
            pltpu.VMEM((8, t), jnp.int32),
            pltpu.SMEM((8, t), jnp.int32),
            pltpu.VMEM((chunk * t, slab), jnp.bfloat16),
            pltpu.SemaphoreType.DMA((nb,)),
            pltpu.SemaphoreType.DMA((nb,)),
            pltpu.SemaphoreType.DMA,
        ],
        cost_estimate=pl.CostEstimate(
            flops=2 * nb * row_tiles * t * slab * width,
            bytes_accessed=nb * (cap * t * t + slab * width) * 2 + 2 * row_tiles * t * width * 4,
            transcendentals=0,
        ),
        name="expand",
    )(*args)
    return out if last else out[0]


def send(a, axis, pairs):
    return lax.ppermute(a, axis, pairs)


def gather_general(packed, major, minor):
    def line(a, step, direction):
        pairs = []
        for i in range(major):
            have = i if direction > 0 else major - 1 - i
            if 0 <= i + direction < major and have >= step - 1:
                pairs += [(i * minor + j, (i + direction) * minor + j) for j in range(minor)]
        return lax.ppermute(a, "col", pairs)

    def turn(a, shift, at):
        return lax.ppermute(a, "col", [(i * minor + j, i * minor + (j + shift) % minor) for i in at for j in range(minor)])

    here = list(range(major))
    waves = [[(packed, here, 0, -1)] + [(turn(packed, s, here), here, s, -1) for s in range(1, minor)]]
    up = down = packed
    for step in range(1, major):
        up, down = line(up, step, 1), line(down, step, -1)
        below = [i - step if i >= step else -1 for i in here]
        above = [i + step if i + step < major else -1 for i in here]
        waves.append([(up, below, 0, -1), (down, above, 0, -1)])
        waves.append([
            (turn(a, s, [i for i in here if at[i] >= 0]), at, s, -1) for a, at in ((up, below), (down, above)) for s in range(1, minor)
        ])
    return waves


def gather_4x2(packed, n_row):
    def z(a, pairs):
        return send(a, "col", [(i * 2 + j, k * 2 + j) for i, k in pairs for j in range(2)])

    def x(a, at):
        return send(a, "col", [(i * 2 + j, i * 2 + 1 - j) for i in at for j in range(2)])

    def some(a, moves, parity):
        return send(a, ("row", "col"), [(r * 8 + i, r * 8 + k) for r in range(parity, n_row, 2) for i, k in moves])

    outer, inner, inward = [(0, 1), (1, 0), (2, 3), (3, 2)], [(1, 2), (2, 1)], [(1, 0), (2, 3)]
    p = z(packed, outer)
    q = z(packed, inner)
    x0 = x(packed, range(4))
    q2 = z(p, inner)
    p2 = z(q, inward)
    xp = x(p, range(4))
    p3 = z(q2, inward)
    xq2 = x(q2, (1, 2))
    xp2 = x(p2, (0, 3))
    e = z(x0, inner)
    f = some(xq2, [(2 + j, j) for j in range(2)] + [(4 + j, 6 + j) for j in range(2)], 0)
    g = some(p3, [(0, 1), (1, 0), (6, 7), (7, 6)], 1)
    return [
        [(packed, [0, 1, 2, 3], 0, -1), (x0, [0, 1, 2, 3], 1, -1), (p, [1, 0, 3, 2], 0, -1), (q, [-1, 2, 1, -1], 0, -1)],
        [(q2, [-1, 3, 0, -1], 0, -1), (p2, [2, -1, -1, 1], 0, -1), (xp, [1, 0, 3, 2], 1, -1)],
        [
            (p3, [3, -1, -1, 0], 0, -1), (e, [-1, 2, 1, -1], 1, -1),
            (xq2, [-1, 3, 0, -1], 1, -1), (xp2, [2, -1, -1, 1], 1, -1),
        ],
        [(f, [3, -1, -1, 0], 1, 0), (g, [3, -1, -1, 0], 1, 1)],
    ]


def body(transition, tile_pattern, kept_tiles):
    row_tiles, col_tiles = tile_pattern.shape
    t = transition.shape[0] // row_tiles
    width = kept_tiles.shape[1] * t
    n_row, n_col = lax.axis_size("row"), lax.axis_size("col")
    major, minor = split_axis(n_col)
    n_y = n_row // 2
    ratio = row_tiles // col_tiles
    r, c = lax.axis_index("row"), lax.axis_index("col")

    packed, panel = pack_tiles(transition, tile_pattern.T, width)
    waves = gather_4x2(packed, n_row) if (major, minor) == (4, 2) else gather_general(packed, major, minor)

    panel = panel.reshape(ratio, col_tiles * t, width)
    pieces = []
    for s in range(n_y):
        there = panel if s == 0 else send(
            panel, "row", [(i * 2 + k, (i + s) % n_y * 2 + k) for i in range(n_y) for k in range(2)])
        pieces += [there, send(there, "row", [(i, i ^ 1) for i in range(n_row)])]

    flat = [entry for wave in waves for entry in wave]
    source = jnp.asarray(np.array([at for _, at, _, _ in flat], np.int32).T)[c // minor]
    parity = jnp.asarray(np.array([only for _, _, _, only in flat], np.int32))
    col = jnp.maximum(source, 0) * minor + (c + minor - jnp.asarray(np.array([s for _, _, s, _ in flat], np.int32))) % minor
    owner = col // ratio
    here = (source >= 0) & ((parity < 0) | (parity == r % 2))
    piece = (r // 2 + n_y - owner // 2) % n_y * 2 + (r + owner) % 2
    meta = jnp.stack([here.astype(jnp.int32), piece, col % ratio], axis=1).astype(jnp.int32)

    acc, first = None, 0
    for w, wave in enumerate(waves):
        last = w == len(waves) - 1
        acc = expand([a for a, _, _, _ in wave], meta, first, pieces, acc, kept_tiles.T if last else None, row_tiles, 4)
        first += len(wave)
    inflated, stats = acc

    bit = 1
    while bit < n_row:
        other = lax.ppermute(stats, "row", [(i, i ^ bit) for i in range(n_row)])
        added = lax.broadcasted_iota(jnp.int32, stats.shape, 0) < 2
        stats = jnp.where(added, stats + other, jnp.maximum(stats, other))
        bit *= 2
    col_sums, squares, col_peaks = stats[0], stats[1], stats[2]
    normalized = inflated / col_sums
    spread = squares / (col_sums * col_sums)
    node_count = transition.shape[0] * n_row
    chaos_value = jnp.full((8, 128), jnp.max(col_peaks / col_sums - spread))
    bit = 1
    while bit < n_col:
        chaos_value = jnp.maximum(chaos_value, lax.ppermute(chaos_value, "col", [(i, i ^ bit) for i in range(n_col)]))
        bit *= 2
    return normalized * node_count, chaos_value[0, 0] * node_count


def solution(mesh):
    placed = (P("row", "col"), P("row", "col"), P("row", "col"))
    step = jax.shard_map(body, mesh=mesh, in_specs=placed, out_specs=(P("row", "col"), P()), check_vma=False)
    if split_axis(mesh.shape["col"]) != (4, 2):
        return step
    return step
```

time: 480 us -> 165 us (0.34)
  waiting for transfers between devices: 401 us -> 74.5 us
  Pallas kernels: 0 us -> 42.3 us
  starting transfers between devices: 0.08 us -> 35.6 us
  blocking collectives: 33.6 us -> 0 us
  matrix products: 15.6 us -> 0 us
  between operations: 15.9 us -> 2.61 us
  local copies, waits for them, and re-layouts: 8.45 us -> 1.89 us
    all_gather x2 -> x0, waiting for transfers between devices: 401 us -> none  [the longest x1 364 us: body(): lax.all_gather(masked, 'col', axis=1, tiled=True)]
    ppermute x0 -> x20, waiting for transfers between devices: none -> 74.5 us  [the longest x15 68 us: send(): return lax.ppermute(a, axis, pairs)]
    pallas_call x0 -> x5, Pallas kernels: none -> 42.3 us  [the longest x4 38.3 us: expand(): pl.pallas_call(kernel, out_shape=out_shape, in_specs=in_specs, out_specs=...]
    ppermute x0 -> x20, starting transfers between devices: none -> 35.6 us  [the longest x15 23.1 us: send(): return lax.ppermute(a, axis, pairs)]
    pmax x2 -> x0, blocking collectives: 27.8 us -> none  [the longest x1 21.4 us: body(): chaos_value = lax.pmax(local_max, 'col')]
    dot_general x1 -> x0, matrix products: 15.6 us -> none  [body(): jnp.dot(lax.all_gather(masked, 'col', axis=1, tiled=True), column_panel,...]
    psum x1 -> x0, blocking collectives: 5.85 us -> none  [body(): lax.psum((jnp.sum(inflated, axis=0), jnp.sum(inflated * inflated, axis=0)...]
    unnamed x9 -> x12, local copies, waits for them, and re-layouts: 5.04 us -> 0.03 us
  transfers between devices with their start and end apart: 2 -> 20, of which waited for: 2 -> 9; matrix products, arithmetic and copies ran while one was open for 0% -> 4% of each run, Pallas kernels for 0% -> 18%
where the time goes in v2:
time: 165 us
  waiting for transfers between devices  74.5 us (45%)
  Pallas kernels  42.3 us (26%)
  starting transfers between devices  35.6 us (22%)
  other arithmetic  7.87 us (5%)
  between operations  2.61 us (2%)
  local copies, waits for them, and re-layouts  1.89 us (1%)
    ppermute x15, waiting for transfers between devices, send(): return lax.ppermute(a, axis, pairs)  68 us
    pallas_call x4, Pallas kernels, expand(): pl.pallas_call(kernel, out_shape=out_shape, in_specs=in_specs, out_specs=...  38.3 us
    ppermute x15, starting transfers between devices, send(): return lax.ppermute(a, axis, pairs)  23.1 us
    ppermute x3, starting transfers between devices, body(): lax.ppermute(chaos_value, 'col', [(i, i ^ bit) for i in range(n_col)])  9.05 us
    pallas_call x1, Pallas kernels, pack_tiles(): pl.pallas_call(kernel, out_shape=(jax.ShapeDtypeStruct((cap * t + NOTE, t...  3.98 us
    ppermute x3, waiting for transfers between devices, body(): lax.ppermute(chaos_value, 'col', [(i, i ^ bit) for i in range(n_col)])  3.45 us
    ppermute x2, starting transfers between devices, body(): other = lax.ppermute(stats, 'row', [(i, i ^ bit) for i in range(n_row)])  3.41 us
  transfers between devices with their start and end apart: 20, of which 9 were waited for; matrix products, arithmetic and copies ran while one was open for 4% of the time, Pallas kernels for 18%

profile of v2, /device:TPU:0, one launch (start us, length us, event | category | flops | bytes accessed | tf_op | source)
XLA Modules:
  0.0 164.7 jit_solution(14917476815663025233)
XLA Ops:
  0.6 0.0 copy-start.5
  0.6 0.0 copy-start.3
  0.7 0.0 copy-start.4
  0.7 4.0 %pack.1 = (bf16[4624,128]{1,0:T(8,128)(2,1)}, bf16[1536,384]{1,0:T(8,128)(2,1)}) custom-call(s32[6,12]{1,0:T(8,128)} %bitcast.25, bf16[1536,768]{1,0:T(8,128)(2,1)} %x_ref.1), custom_call_target="tpu_custom_call" | custom-call | bytes 4718592 | tf_op jit(solution)/shard_map/pack/pallas_call | solution.py:45
  4.7 3.1 %collective-permute-start = (bf16[4624,128]{1,0:T(8,128)(2,1)}, bf16[4624,128]{1,0:T(8,128)(2,1)}, u32[]{:S(2)}, u32[]{:S(2)}) collective-permute-start(bf16[4624,128]{1,0:T(8,128)(2,1)} %get-tuple-element.6.refs_1_), channel_id=1, source_target_pairs={{0,2},{1,3},{2,0},{3,1},{4,6},{5,7},{6,4},{7,5},{8,10},{9,11},{10,... | collective-permute-start | bytes 3551240 | tf_op jit(solution)/shard_map/ppermute | solution.py:184
  7.7 1.7 %collective-permute-start.11 = (bf16[4624,128]{1,0:T(8,128)(2,1)}, bf16[4624,128]{1,0:T(8,128)(2,1)}, u32[]{:S(2)}, u32[]{:S(2)}) collective-permute-start(bf16[4624,128]{1,0:T(8,128)(2,1)} %get-tuple-element.6.refs_1_), channel_id=1, source_target_pairs={{2,4},{3,5},{4,2},{5,3},{10,12},{11,13},{12,10},{13,11},{18,20},{1... | collective-permute-start | bytes 3551240 | tf_op jit(solution)/shard_map/ppermute | solution.py:184
  9.4 1.5 collective-permute-start.7
  10.9 23.1 %collective-permute-done.refs_3_ = bf16[4624,128]{1,0:T(8,128)(2,1)} collective-permute-done((bf16[4624,128]{1,0:T(8,128)(2,1)}, bf16[4624,128]{1,0:T(8,128)(2,1)}, u32[]{:S(2)}, u32[]{:S(2)}) %collective-permute-start) | collective-permute-done | bytes 1183776 | tf_op jit(solution)/shard_map/ppermute | solution.py:184
  34.1 1.7 %collective-permute-start.1 = (bf16[4624,128]{1,0:T(8,128)(2,1)}, bf16[4624,128]{1,0:T(8,128)(2,1)}, u32[]{:S(2)}, u32[]{:S(2)}) collective-permute-start(bf16[4624,128]{1,0:T(8,128)(2,1)} %collective-permute-done.refs_3_), channel_id=1, source_target_pairs={{2,4},{3,5},{4,2},{5,3},{10,12},{11,13},{12,10},{13,11},{18,20},{1... | collective-permute-start | bytes 3551240 | tf_op jit(solution)/shard_map/ppermute | solution.py:184
  35.8 1.7 %collective-permute-start.9 = (bf16[4624,128]{1,0:T(8,128)(2,1)}, bf16[4624,128]{1,0:T(8,128)(2,1)}, u32[]{:S(2)}, u32[]{:S(2)}) collective-permute-start(bf16[4624,128]{1,0:T(8,128)(2,1)} %get-tuple-element.6.refs_1_), channel_id=1, source_target_pairs={{0,1},{1,0},{2,3},{3,2},{4,5},{5,4},{6,7},{7,6},{8,9},{9,8},{10,11... | collective-permute-start | bytes 3551240 | tf_op jit(solution)/shard_map/ppermute | solution.py:184
  37.5 1.3 collective-permute-start.12
  38.8 0.0 collective-permute-done.7.refs_7_.refs_6_
  38.8 0.3 collective-permute-start.8
  39.1 1.7 %collective-permute-start.2 = (bf16[4624,128]{1,0:T(8,128)(2,1)}, bf16[4624,128]{1,0:T(8,128)(2,1)}, u32[]{:S(2)}, u32[]{:S(2)}) collective-permute-start(bf16[4624,128]{1,0:T(8,128)(2,1)} %collective-permute-done.1.refs_1_), channel_id=1, source_target_pairs={{2,3},{3,2},{4,5},{5,4},{10,11},{11,10},{12,13},{13,12},{18,19},{1... | collective-permute-start | bytes 3551240 | tf_op jit(solution)/shard_map/ppermute | solution.py:184
  40.8 1.3 collective-permute-start.4
  42.1 22.4 %collective-permute-done.9.refs_2_ = bf16[4624,128]{1,0:T(8,128)(2,1)} collective-permute-done((bf16[4624,128]{1,0:T(8,128)(2,1)}, bf16[4624,128]{1,0:T(8,128)(2,1)}, u32[]{:S(2)}, u32[]{:S(2)}) %collective-permute-start.9) | collective-permute-done | bytes 1183776 | tf_op jit(solution)/shard_map/ppermute | solution.py:184
  64.5 1.7 %collective-permute-start.14 = (bf16[4624,128]{1,0:T(8,128)(2,1)}, bf16[4624,128]{1,0:T(8,128)(2,1)}, u32[]{:S(2)}, u32[]{:S(2)}) collective-permute-start(bf16[4624,128]{1,0:T(8,128)(2,1)} %collective-permute-done.refs_3_), channel_id=1, source_target_pairs={{0,1},{1,0},{2,3},{3,2},{4,5},{5,4},{6,7},{7,6},{8,9},{9,8},{10,11... | collective-permute-start | bytes 3551240 | tf_op jit(solution)/shard_map/ppermute | solution.py:184
  66.3 1.7 %collective-permute-start.10 = (bf16[4624,128]{1,0:T(8,128)(2,1)}, bf16[4624,128]{1,0:T(8,128)(2,1)}, u32[]{:S(2)}, u32[]{:S(2)}) collective-permute-start(bf16[4624,128]{1,0:T(8,128)(2,1)} %collective-permute-done.9.refs_2_), channel_id=1, source_target_pairs={{2,4},{3,5},{4,2},{5,3},{10,12},{11,13},{12,10},{13,11},{18,20},{1... | collective-permute-start | bytes 3551240 | tf_op jit(solution)/shard_map/ppermute | solution.py:184
  68.0 1.2 collective-permute-done.12.refs_2_
  69.2 2.4 %collective-permute-start.13 = (bf16[4624,128]{1,0:T(8,128)(2,1)}, bf16[4624,128]{1,0:T(8,128)(2,1)}, u32[]{:S(2)}, u32[]{:S(2)}) collective-permute-start(bf16[4624,128]{1,0:T(8,128)(2,1)} %collective-permute-done.12.refs_2_), channel_id=1, source_target_pairs={{0,1},{1,0},{6,7},{7,6},{8,9},{9,8},{14,15},{15,14},{16,17},{17,16... | collective-permute-start | bytes 3551240 | tf_op jit(solution)/shard_map/ppermute | solution.py:184
  71.6 1.2 fusion.9
  72.8 1.3 collective-permute-start.3
  74.1 20.2 %collective-permute-done.4.refs_1_ = bf16[4624,128]{1,0:T(8,128)(2,1)} collective-permute-done((bf16[4624,128]{1,0:T(8,128)(2,1)}, bf16[4624,128]{1,0:T(8,128)(2,1)}, u32[]{:S(2)}, u32[]{:S(2)}) %collective-permute-start.4) | collective-permute-done | bytes 1183776 | tf_op jit(solution)/shard_map/ppermute | solution.py:184
  94.3 1.7 %collective-permute-start.5 = (bf16[4624,128]{1,0:T(8,128)(2,1)}, bf16[4624,128]{1,0:T(8,128)(2,1)}, u32[]{:S(2)}, u32[]{:S(2)}) collective-permute-start(bf16[4624,128]{1,0:T(8,128)(2,1)} %collective-permute-done.4.refs_1_), channel_id=1, source_target_pairs={{8,9},{9,8},{14,15},{15,14},{24,25},{25,24},{30,31},{31,30}} | collective-permute-start | bytes 3551240 | tf_op jit(solution)/shard_map/ppermute | solution.py:184
  96.1 0.7 fusion.5
  96.7 0.7 copy.14.refs_0_
  97.4 11.1 %expand.4.refs_8_ = f32[1536,384]{1,0:T(8,128)} custom-call(s32[13,3]{1,0:T(8,128)} %copy.14.refs_0_, bf16[4624,128]{1,0:T(8,128)(2,1)} %get-tuple-element.6.refs_1_, bf16[4624,128]{1,0:T(8,128)(2,1)} %collective-permute-done.9.refs_2_, bf16[4624,128]{1,0:T(8,128)(2,1)} %collective-permute-done.refs_3_, bf16[4624,128]{1,0:T(8,128)(2,1)} %collective-permute-done.11.refs_4_, ...), custom_call_target="tpu_custom_call" | custom-call | flops 3623878656 | bytes 11796480 | tf_op jit(solution)/shard_map/expand/pallas_call | solution.py:158
  108.6 9.6 %expand.5.refs_9_ = f32[1536,384]{1,0:T(8,128)} custom-call(s32[13,3]{1,0:T(8,128)} %copy.14.refs_0_, bf16[4624,128]{1,0:T(8,128)(2,1)} %collective-permute-done.1.refs_1_, bf16[4624,128]{1,0:T(8,128)(2,1)} %collective-permute-done.12.refs_2_, bf16[4624,128]{1,0:T(8,128)(2,1)} %collective-permute-done.14.refs_3_, bf16[2,768,384]{2,1,0:T(8,128)(2,1)} %bitcast.22, ...), custom_call_target="tpu_custom_call" | custom-call | flops 2717908992 | bytes 10027008 | tf_op jit(solution)/shard_map/expand/pallas_call | solution.py:158
  118.2 0.9 collective-permute-done.13.refs_4_
  119.2 9.5 %expand.6.refs_8_ = f32[1536,384]{1,0:T(8,128)} custom-call(s32[13,3]{1,0:T(8,128)} %copy.14.refs_0_, bf16[4624,128]{1,0:T(8,128)(2,1)} %collective-permute-done.4.refs_1_, bf16[4624,128]{1,0:T(8,128)(2,1)} %collective-permute-done.10.refs_2_, bf16[4624,128]{1,0:T(8,128)(2,1)} %collective-permute-done.2.refs_3_, ...), custom_call_target="tpu_custom_call" | custom-call | flops 3623878656 | bytes 11796480 | tf_op jit(solution)/shard_map/expand/pallas_call | solution.py:158
  128.7 8.0 %expand.7 = (f32[1536,384]{1,0:T(8,128)}, f32[8,384]{1,0:T(8,128)}) custom-call(s32[13,3]{1,0:T(8,128)} %copy.14.refs_0_, s32[3,12]{1,0:T(4,128)} %bitcast.26, bf16[4624,128]{1,0:T(8,128)(2,1)} %collective-permute-done.3.refs_2_, bf16[4624,128]{1,0:T(8,128)(2,1)} %collective-permute-done.5.refs_3_, bf16[2,768,384]{2,1,0:T(8,128)(2,1)} %bitcast.24, ...), custom_call_target="tpu_custom_call" | custom-call | flops 1811939328 | bytes 8257536 | tf_op jit(solution)/shard_map/expand/pallas_call | solution.py:158
  136.7 1.7 %collective-permute-start.15 = (f32[8,384]{1,0:T(8,128)}, f32[8,384]{1,0:T(8,128)S(1)}, u32[]{:S(2)}, u32[]{:S(2)}) collective-permute-start(f32[8,384]{1,0:T(8,128)} %get-tuple-element.9), channel_id=1, source_target_pairs={{0,8},{8,0},{16,24},{24,16},{1,9},{9,1},{17,25},{25,17},{2,10},{10... | collective-permute-start | bytes 36872 | tf_op jit(solution)/shard_map/ppermute | solution.py:285
  138.5 1.0 collective-permute-done.15
  139.5 0.8 maximum_select_fusion.1
  140.3 1.7 %collective-permute-start.16 = (f32[8,384]{1,0:T(8,128)S(1)}, f32[8,384]{1,0:T(8,128)S(1)}, u32[]{:S(2)}, u32[]{:S(2)}) collective-permute-start(f32[8,384]{1,0:T(8,128)S(1)} %maximum_select_fusion.1), channel_id=1, source_target_pairs={{0,16},{8,24},{16,0},{24,8},{1,17},{9,25},{17,1},{25,9},{2,18},{10... | collective-permute-start | bytes 36872 | tf_op jit(solution)/shard_map/ppermute | solution.py:285
  141.9 2.0 %collective-permute-done.16 = f32[8,384]{1,0:T(8,128)S(1)} collective-permute-done((f32[8,384]{1,0:T(8,128)S(1)}, f32[8,384]{1,0:T(8,128)S(1)}, u32[]{:S(2)}, u32[]{:S(2)}) %collective-permute-start.16) | collective-permute-done | bytes 12320 | tf_op jit(solution)/shard_map/ppermute | solution.py:285
  144.0 0.1 maximum_select_fusion
  144.1 0.6 subtract_reduce_fusion
  144.7 0.6 broadcast_in_dim.3
  145.3 1.8 %collective-permute-start.17 = (f32[8,128]{1,0:T(8,128)S(1)}, f32[8,128]{1,0:T(8,128)S(1)}, u32[]{:S(2)}, u32[]{:S(2)}) collective-permute-start(f32[8,128]{1,0:T(8,128)S(1)} %broadcast_in_dim.3), channel_id=1, source_target_pairs={{0,1},{1,0},{2,3},{3,2},{4,5},{5,4},{6,7},{7,6},{8,9},{9,8},{10,11... | collective-permute-start | bytes 12296 | tf_op jit(solution)/shard_map/ppermute | solution.py:296
  147.2 1.9 %collective-permute-done.17 = f32[8,128]{1,0:T(8,128)S(1)} collective-permute-done((f32[8,128]{1,0:T(8,128)S(1)}, f32[8,128]{1,0:T(8,128)S(1)}, u32[]{:S(2)}, u32[]{:S(2)}) %collective-permute-start.17) | collective-permute-done | bytes 4128 | tf_op jit(solution)/shard_map/ppermute | solution.py:296
  149.0 0.6 broadcast_maximum_fusion
  149.7 4.4 %collective-permute-start.18 = (f32[8,128]{1,0:T(8,128)S(1)}, f32[8,128]{1,0:T(8,128)S(1)}, u32[]{:S(2)}, u32[]{:S(2)}) collective-permute-start(f32[8,128]{1,0:T(8,128)S(1)} %broadcast_maximum_fusion), channel_id=1, source_target_pairs={{0,2},{1,3},{2,0},{3,1},{4,6},{5,7},{6,4},{7,5},{8,10},{9,11},{10,... | collective-permute-start | bytes 12296 | tf_op jit(solution)/shard_map/ppermute | solution.py:296
  154.1 1.6 collective-permute-done.18
  155.7 0.6 fusion.11
  156.3 2.8 %collective-permute-start.19 = (f32[8,128]{1,0:T(8,128)S(1)}, f32[8,128]{1,0:T(8,128)S(1)}, u32[]{:S(2)}, u32[]{:S(2)}) collective-permute-start(f32[8,128]{1,0:T(8,128)S(1)} %fusion.11), channel_id=1, source_target_pairs={{0,4},{1,5},{2,6},{3,7},{4,0},{5,1},{6,2},{7,3},{8,12},{9,13},{10,... | collective-permute-start | bytes 12296 | tf_op jit(solution)/shard_map/ppermute | solution.py:296
  159.2 3.2 %divide_multiply_fusion = f32[1536,384]{1,0:T(8,128)} fusion(f32[1536,384]{1,0:T(8,128)} %get-tuple-element.8, f32[384]{0:T(512)S(1)} %get-tuple-element.12), kind=kLoop, calls=%fused_computation | loop fusion | flops 1179648 | bytes 4720128 | tf_op jit(solution)/shard_map/mul | solution.py:298
  162.4 0.5 slice.15
  (25 shorter events, 0.1 us)
Async XLA Ops:
  0.6 71.0 %copy-start.5 = (s32[4,13]{1,0:T(4,128)S(1)}, s32[4,13]{1,0:T(4,128)}, u32[]{:S(2)}) copy-start(s32[4,13]{1,0:T(4,128)} %constant.97.clone) | copy-start | bytes 628
  0.6 72.2 %copy-start.3 = (pred[13]{0:T(512)(128)(4,1)S(1)}, pred[13]{0:T(512)(128)(4,1)}, u32[]{:S(2)}) copy-start(pred[13]{0:T(512)(128)(4,1)} %constant.102) | copy-start | bytes 43
  0.7 72.2 %copy-start.4 = (s32[13]{0:T(128)S(1)}, s32[13]{0:T(128)}, u32[]{:S(2)}) copy-start(s32[13]{0:T(128)} %constant.98.clone) | copy-start | bytes 160
  4.7 29.4 %collective-permute-start = (bf16[4624,128]{1,0:T(8,128)(2,1)}, bf16[4624,128]{1,0:T(8,128)(2,1)}, u32[]{:S(2)}, u32[]{:S(2)}) collective-permute-start(bf16[4624,128]{1,0:T(8,128)(2,1)} %get-tuple-element.6.refs_1_), channel_id=1, source_target_pairs={{0,2},{1,3},{2,0},{3,1},{4,6},{5,7},{6,4},{7,5},{8,10},{9,11},{10,... | collective-permute-start | bytes 3551240 | tf_op jit(solution)/shard_map/ppermute | solution.py:184
  7.7 29.8 %collective-permute-start.11 = (bf16[4624,128]{1,0:T(8,128)(2,1)}, bf16[4624,128]{1,0:T(8,128)(2,1)}, u32[]{:S(2)}, u32[]{:S(2)}) collective-permute-start(bf16[4624,128]{1,0:T(8,128)(2,1)} %get-tuple-element.6.refs_1_), channel_id=1, source_target_pairs={{2,4},{3,5},{4,2},{5,3},{10,12},{11,13},{12,10},{13,11},{18,20},{1... | collective-permute-start | bytes 3551240 | tf_op jit(solution)/shard_map/ppermute | solution.py:184
  9.4 29.4 %collective-permute-start.7 = (bf16[2,768,384]{2,1,0:T(8,128)(2,1)}, bf16[2,768,384]{2,1,0:T(8,128)(2,1)S(1)}, u32[]{:S(2)}, u32[]{:S(2)}) collective-permute-start(bf16[2,768,384]{2,1,0:T(8,128)(2,1)} %bitcast.19), channel_id=1, source_target_pairs={{0,16},{8,24},{16,0},{24,8},{1,17},{9,25},{17,1},{25,9},{2,18},{10... | collective-permute-start | bytes 3538952 | tf_op jit(solution)/shard_map/ppermute | solution.py:184
  34.1 5.1 %collective-permute-start.1 = (bf16[4624,128]{1,0:T(8,128)(2,1)}, bf16[4624,128]{1,0:T(8,128)(2,1)}, u32[]{:S(2)}, u32[]{:S(2)}) collective-permute-start(bf16[4624,128]{1,0:T(8,128)(2,1)} %collective-permute-done.refs_3_), channel_id=1, source_target_pairs={{2,4},{3,5},{4,2},{5,3},{10,12},{11,13},{12,10},{13,11},{18,20},{1... | collective-permute-start | bytes 3551240 | tf_op jit(solution)/shard_map/ppermute | solution.py:184
  35.8 5.1 %collective-permute-start.6 = (bf16[2,768,384]{2,1,0:T(8,128)(2,1)}, bf16[2,768,384]{2,1,0:T(8,128)(2,1)S(1)}, u32[]{:S(2)}, u32[]{:S(2)}) collective-permute-start(bf16[2,768,384]{2,1,0:T(8,128)(2,1)} %bitcast.20), channel_id=1, source_target_pairs={{0,8},{8,0},{16,24},{24,16},{1,9},{9,1},{17,25},{25,17},{2,10},{10... | collective-permute-start | bytes 3538952 | tf_op jit(solution)/shard_map/ppermute | solution.py:184
  35.8 28.8 %collective-permute-start.9 = (bf16[4624,128]{1,0:T(8,128)(2,1)}, bf16[4624,128]{1,0:T(8,128)(2,1)}, u32[]{:S(2)}, u32[]{:S(2)}) collective-permute-start(bf16[4624,128]{1,0:T(8,128)(2,1)} %get-tuple-element.6.refs_1_), channel_id=1, source_target_pairs={{0,1},{1,0},{2,3},{3,2},{4,5},{5,4},{6,7},{7,6},{8,9},{9,8},{10,11... | collective-permute-start | bytes 3551240 | tf_op jit(solution)/shard_map/ppermute | solution.py:184
  37.5 31.7 %collective-permute-start.12 = (bf16[4624,128]{1,0:T(8,128)(2,1)}, bf16[4624,128]{1,0:T(8,128)(2,1)}, u32[]{:S(2)}, u32[]{:S(2)}) collective-permute-start(bf16[4624,128]{1,0:T(8,128)(2,1)} %collective-permute-done.11.refs_4_), channel_id=1, source_target_pairs={{2,0},{3,1},{4,6},{5,7},{10,8},{11,9},{12,14},{13,15},{18,16},{19,... | collective-permute-start | bytes 3551240 | tf_op jit(solution)/shard_map/ppermute | solution.py:184
  38.8 58.6 %copy-start = (bf16[2,768,384]{2,1,0:T(8,128)(2,1)}, bf16[2,768,384]{2,1,0:T(8,128)(2,1)S(1)}, u32[]{:S(2)}) copy-start(bf16[2,768,384]{2,1,0:T(8,128)(2,1)S(1)} %collective-permute-done.7.refs_7_.refs_6_) | copy-start | bytes 3538948
  38.8 27.5 %collective-permute-start.8 = (bf16[2,768,384]{2,1,0:T(8,128)(2,1)S(1)}, bf16[2,768,384]{2,1,0:T(8,128)(2,1)S(1)}, u32[]{:S(2)}, u32[]{:S(2)}) collective-permute-start(bf16[2,768,384]{2,1,0:T(8,128)(2,1)S(1)} %collective-permute-done.7.refs_7_.refs_6_), channel_id=1, source_target_pairs={{0,8},{8,0},{16,24},{24,16},{1,9},{9,1},{17,25},{25,17},{2,10},{10... | collective-permute-start | bytes 3538952 | tf_op jit(solution)/shard_map/ppermute | solution.py:184
  39.1 33.7 %collective-permute-start.2 = (bf16[4624,128]{1,0:T(8,128)(2,1)}, bf16[4624,128]{1,0:T(8,128)(2,1)}, u32[]{:S(2)}, u32[]{:S(2)}) collective-permute-start(bf16[4624,128]{1,0:T(8,128)(2,1)} %collective-permute-done.1.refs_1_), channel_id=1, source_target_pairs={{2,3},{3,2},{4,5},{5,4},{10,11},{11,10},{12,13},{13,12},{18,19},{1... | collective-permute-start | bytes 3551240 | tf_op jit(solution)/shard_map/ppermute | solution.py:184
  40.8 56.6 %copy-start.1 = (bf16[2,768,384]{2,1,0:T(8,128)(2,1)}, bf16[2,768,384]{2,1,0:T(8,128)(2,1)S(1)}, u32[]{:S(2)}) copy-start(bf16[2,768,384]{2,1,0:T(8,128)(2,1)S(1)} %collective-permute-done.6.refs_6_.refs_5_) | copy-start | bytes 3538948
  40.8 53.5 %collective-permute-start.4 = (bf16[4624,128]{1,0:T(8,128)(2,1)}, bf16[4624,128]{1,0:T(8,128)(2,1)}, u32[]{:S(2)}, u32[]{:S(2)}) collective-permute-start(bf16[4624,128]{1,0:T(8,128)(2,1)} %collective-permute-done.1.refs_1_), channel_id=1, source_target_pairs={{2,0},{3,1},{4,6},{5,7},{10,8},{11,9},{12,14},{13,15},{18,16},{19,... | collective-permute-start | bytes 3551240 | tf_op jit(solution)/shard_map/ppermute | solution.py:184
  64.5 44.0 %collective-permute-start.14 = (bf16[4624,128]{1,0:T(8,128)(2,1)}, bf16[4624,128]{1,0:T(8,128)(2,1)}, u32[]{:S(2)}, u32[]{:S(2)}) collective-permute-start(bf16[4624,128]{1,0:T(8,128)(2,1)} %collective-permute-done.refs_3_), channel_id=1, source_target_pairs={{0,1},{1,0},{2,3},{3,2},{4,5},{5,4},{6,7},{7,6},{8,9},{9,8},{10,11... | collective-permute-start | bytes 3551240 | tf_op jit(solution)/shard_map/ppermute | solution.py:184
  66.3 31.1 %copy-start.2 = (bf16[2,768,384]{2,1,0:T(8,128)(2,1)}, bf16[2,768,384]{2,1,0:T(8,128)(2,1)S(1)}, u32[]{:S(2)}) copy-start(bf16[2,768,384]{2,1,0:T(8,128)(2,1)S(1)} %collective-permute-done.8.refs_8_.refs_7_) | copy-start | bytes 3538948
  66.3 51.9 %collective-permute-start.10 = (bf16[4624,128]{1,0:T(8,128)(2,1)}, bf16[4624,128]{1,0:T(8,128)(2,1)}, u32[]{:S(2)}, u32[]{:S(2)}) collective-permute-start(bf16[4624,128]{1,0:T(8,128)(2,1)} %collective-permute-done.9.refs_2_), channel_id=1, source_target_pairs={{2,4},{3,5},{4,2},{5,3},{10,12},{11,13},{12,10},{13,11},{18,20},{1... | collective-permute-start | bytes 3551240 | tf_op jit(solution)/shard_map/ppermute | solution.py:184
  69.2 49.9 %collective-permute-start.13 = (bf16[4624,128]{1,0:T(8,128)(2,1)}, bf16[4624,128]{1,0:T(8,128)(2,1)}, u32[]{:S(2)}, u32[]{:S(2)}) collective-permute-start(bf16[4624,128]{1,0:T(8,128)(2,1)} %collective-permute-done.12.refs_2_), channel_id=1, source_target_pairs={{0,1},{1,0},{6,7},{7,6},{8,9},{9,8},{14,15},{15,14},{16,17},{17,16... | collective-permute-start | bytes 3551240 | tf_op jit(solution)/shard_map/ppermute | solution.py:184
  72.8 55.8 %collective-permute-start.3 = (bf16[4624,128]{1,0:T(8,128)(2,1)}, bf16[4624,128]{1,0:T(8,128)(2,1)}, u32[]{:S(2)}, u32[]{:S(2)}) collective-permute-start(bf16[4624,128]{1,0:T(8,128)(2,1)} %collective-permute-done.2.refs_3_), channel_id=1, source_target_pairs={{2,0},{3,1},{4,6},{5,7},{18,16},{19,17},{20,22},{21,23}} | collective-permute-start | bytes 3551240 | tf_op jit(solution)/shard_map/ppermute | solution.py:184
  94.3 34.3 %collective-permute-start.5 = (bf16[4624,128]{1,0:T(8,128)(2,1)}, bf16[4624,128]{1,0:T(8,128)(2,1)}, u32[]{:S(2)}, u32[]{:S(2)}) collective-permute-start(bf16[4624,128]{1,0:T(8,128)(2,1)} %collective-permute-done.4.refs_1_), channel_id=1, source_target_pairs={{8,9},{9,8},{14,15},{15,14},{24,25},{25,24},{30,31},{31,30}} | collective-permute-start | bytes 3551240 | tf_op jit(solution)/shard_map/ppermute | solution.py:184
  136.7 2.8 %collective-permute-start.15 = (f32[8,384]{1,0:T(8,128)}, f32[8,384]{1,0:T(8,128)S(1)}, u32[]{:S(2)}, u32[]{:S(2)}) collective-permute-start(f32[8,384]{1,0:T(8,128)} %get-tuple-element.9), channel_id=1, source_target_pairs={{0,8},{8,0},{16,24},{24,16},{1,9},{9,1},{17,25},{25,17},{2,10},{10... | collective-permute-start | bytes 36872 | tf_op jit(solution)/shard_map/ppermute | solution.py:285
  140.3 3.7 %collective-permute-start.16 = (f32[8,384]{1,0:T(8,128)S(1)}, f32[8,384]{1,0:T(8,128)S(1)}, u32[]{:S(2)}, u32[]{:S(2)}) collective-permute-start(f32[8,384]{1,0:T(8,128)S(1)} %maximum_select_fusion.1), channel_id=1, source_target_pairs={{0,16},{8,24},{16,0},{24,8},{1,17},{9,25},{17,1},{25,9},{2,18},{10... | collective-permute-start | bytes 36872 | tf_op jit(solution)/shard_map/ppermute | solution.py:285
  145.3 3.7 %collective-permute-start.17 = (f32[8,128]{1,0:T(8,128)S(1)}, f32[8,128]{1,0:T(8,128)S(1)}, u32[]{:S(2)}, u32[]{:S(2)}) collective-permute-start(f32[8,128]{1,0:T(8,128)S(1)} %broadcast_in_dim.3), channel_id=1, source_target_pairs={{0,1},{1,0},{2,3},{3,2},{4,5},{5,4},{6,7},{7,6},{8,9},{9,8},{10,11... | collective-permute-start | bytes 12296 | tf_op jit(solution)/shard_map/ppermute | solution.py:296
  149.7 6.0 %collective-permute-start.18 = (f32[8,128]{1,0:T(8,128)S(1)}, f32[8,128]{1,0:T(8,128)S(1)}, u32[]{:S(2)}, u32[]{:S(2)}) collective-permute-start(f32[8,128]{1,0:T(8,128)S(1)} %broadcast_maximum_fusion), channel_id=1, source_target_pairs={{0,2},{1,3},{2,0},{3,1},{4,6},{5,7},{6,4},{7,5},{8,10},{9,11},{10,... | collective-permute-start | bytes 12296 | tf_op jit(solution)/shard_map/ppermute | solution.py:296
  156.3 6.1 %collective-permute-start.19 = (f32[8,128]{1,0:T(8,128)S(1)}, f32[8,128]{1,0:T(8,128)S(1)}, u32[]{:S(2)}, u32[]{:S(2)}) collective-permute-start(f32[8,128]{1,0:T(8,128)S(1)} %fusion.11), channel_id=1, source_target_pairs={{0,4},{1,5},{2,6},{3,7},{4,0},{5,1},{6,2},{7,3},{8,12},{9,13},{10,... | collective-permute-start | bytes 12296 | tf_op jit(solution)/shard_map/ppermute | solution.py:296
